TPU v7x, 768 devices: a whole 4x8x12 slice. The times are simulated.
768 devices in a mesh: slab: 96 (over z, x, core), depth: 8 (over y).
Axes of the slice: x: 4, y: 8, z: 12, core: 2. Of those that a mesh axis runs over, the one named last changes fastest.
Arguments:
- nutrient: float32 [768, 256, 512], P('slab', 'depth'), may hold values from 0.5 to 2
- species: bfloat16 [786432, 128], P(('slab', 'depth')), may hold values from -6 to 6
- agent_cell: int32 [786432], P(('slab', 'depth')), may hold values from 0 to 131071
- death_flag: int32 [786432], P(('slab', 'depth')), may hold values 0 or 1
- divide_flag: int32 [786432], P(('slab', 'depth')), may hold values 0 or 1
- slab_move: int32 [786432], P(('slab', 'depth')), may hold values from 0 to 2, as said below
- depth_route: int32 [786432, 1], P(('slab', 'depth')), may hold values from 0 to 7; in each aligned block of 1024 rows (0 to 1023, 1024 to 2047, ...) at most 256 rows name the same one
- net_weight: bfloat16 [128, 128], replicated, may hold values from -0.5 to 0.5
- sensing: float32 [128], replicated, may hold values from -1 to 1
- uptake_weight: bfloat16 [128], replicated, may hold values from -0.5 to 0.5
Outputs:
- nutrient_next: float32 [768, 256, 512], P('slab', 'depth')
- species_after_step: bfloat16 [1769472, 128], P(('slab', 'depth'))
Inputs may be any that keep to these rules, and one draw needn't show every extreme that they name: `slab_move`: within each device's 1024 rows at most 128 carry 1 and at most 128 carry 2; some device has exactly 128 carrying 1 and some device exactly 128 carrying 2. `depth_route`: within each device's 1024 rows no depth index is named more than 256 times; one is named exactly 256 times in some device.
All inputs are finite; a program needn't handle non-finite values. No bound on the sum of `death_flag` or of `divide_flag` on one device may be relied on, other than what follows from the above.
Results may differ from a plain program's by a relative error of at most 0.0045.
Values may be sent and summed in bfloat16 or wider, within the bound.
A program may use at most 128 MiB of HBM per device.

v0:
```python
import jax
import jax.numpy as jnp
from jax import lax
from jax.sharding import PartitionSpec as P

PRE = 2
COARSE = 4
MIG = 128


SCREENING = 0.05
DAMPING = 2.0 / 3.0


def extended(block, sides, width, periodic):
    for axis, dim in sides:
        count = lax.axis_size(axis)
        forward = [(i, i + 1) for i in range(count - 1)]
        if periodic:
            forward.append((count - 1, 0))
        backward = [(target, source) for source, target in forward]
        low = lax.ppermute(
            lax.slice_in_dim(block, block.shape[dim] - width, None, axis=dim), axis, forward
        )
        high = lax.ppermute(lax.slice_in_dim(block, 0, width, axis=dim), axis, backward)
        block = jnp.concatenate([low, block, high], axis=dim)
    return block


def passed_along(array, axis, by):
    count = lax.axis_size(axis)
    return lax.ppermute(array, axis, [(i, (i + by) % count) for i in range(count)])


def neighbours(grid_field):
    first_padded = extended(grid_field.astype(jnp.bfloat16), (("slab", 0),), 1, True).astype(
        grid_field.dtype
    )
    neighbour_total = first_padded[2:] + first_padded[:-2]
    second_padded = extended(grid_field.astype(jnp.bfloat16), (("depth", 1),), 1, False).astype(
        grid_field.dtype
    )
    neighbour_total = neighbour_total + second_padded[:, 2:] + second_padded[:, :-2]
    third_padded = jnp.pad(grid_field, ((0, 0), (0, 0), (1, 1)))
    return neighbour_total + third_padded[:, :, 2:] + third_padded[:, :, :-2]


def relax_step(grid_field, target, centre):
    image_field = centre * grid_field - neighbours(grid_field)
    return grid_field + DAMPING * (target - image_field) / centre


def smooth_phase(grid_field, target, centre):
    for sweep_step in range(PRE):
        grid_field = relax_step(grid_field, target, centre)
    return grid_field


def network_update(row_block, sensed_level, keep_mask, net_weight, sensing):
    activation = jnp.dot(row_block, net_weight, preferred_element_type=jnp.float32)
    activation = activation + sensed_level.astype(jnp.float32)[..., None] * sensing
    return (
        keep_mask[..., None] * (0.5 * row_block.astype(jnp.float32) + jnp.tanh(activation))
    ).astype(jnp.bfloat16)


def local(
    nutrient,
    species,
    agent_cell,
    death_flag,
    divide_flag,
    slab_move,
    depth_route,
    net_weight,
    sensing,
    uptake_weight,
):
    depths = lax.axis_size("depth")
    rows_here = species.shape[0]
    capacity = 2 * rows_here // depths
    width = species.shape[1]
    flat_field = nutrient.reshape(-1)
    sample = flat_field[agent_cell]
    alive_mask = (1 - death_flag).astype(jnp.float32)
    uptake_score = jnp.dot(species, uptake_weight, preferred_element_type=jnp.float32)
    uptake = (
        alive_mask
        * (1.0 + divide_flag.astype(jnp.float32))
        * jax.nn.softplus(uptake_score)
        * sample
        / (0.5 + sample)
    )
    source = jnp.zeros_like(flat_field).at[agent_cell].add(uptake).reshape(nutrient.shape)
    sensed = sample.astype(jnp.bfloat16)
    stay_mask = slab_move == 0
    target_device = depth_route[:, 0]
    dest_hits = (target_device[:, None] == jnp.arange(depths, dtype=jnp.int32)[None, :]).astype(
        jnp.int32
    )
    earlier = jnp.cumsum(dest_hits, axis=0) - dest_hits
    destination_slot = jnp.sum(earlier * dest_hits, axis=1)
    outgoing = []
    updated = network_update(species, sensed, alive_mask, net_weight, sensing)
    remaining_agents = jnp.where(stay_mask[:, None], updated, jnp.zeros_like(updated))
    packed = (
        jnp.zeros((depths, capacity, width), jnp.bfloat16)
        .at[target_device, destination_slot]
        .set(remaining_agents)
    )
    arrived = lax.all_to_all(packed, "depth", split_axis=0, concat_axis=0, tiled=True)
    for move_code in (1, 2):
        chosen = (slab_move == move_code).astype(jnp.int32)
        rank_order = jnp.cumsum(chosen) - chosen
        outgoing.append(
            jnp.zeros((MIG, width), jnp.bfloat16)
            .at[jnp.where(chosen == 1, rank_order, MIG)]
            .set(updated, mode="drop")
        )
    arrivals = []
    for shift_by, buffer in ((1, outgoing[0]), (-1, outgoing[1])):
        arrivals.append(passed_along(buffer, "slab", shift_by))
    species_after_step = jnp.concatenate(
        [arrived.reshape(depths * capacity, width), arrivals[0], arrivals[1]], axis=0
    )
    centre = 6.0 + SCREENING
    target = SCREENING * nutrient - source
    grid_field = smooth_phase(nutrient, target, centre)
    residual = target - (centre * grid_field - neighbours(grid_field))
    first_cells, second_cells, third_cells = residual.shape
    coarse_target = 4.0 * residual.reshape(
        first_cells // 2, 2, second_cells // 2, 2, third_cells // 2, 2
    ).mean(axis=(1, 3, 5))
    coarse_centre = 6.0 + 4.0 * SCREENING
    coarse = jnp.zeros_like(coarse_target)
    for sweep_step in range(COARSE):
        coarse = relax_step(coarse, coarse_target, coarse_centre)
    grid_field = grid_field + jnp.repeat(jnp.repeat(jnp.repeat(coarse, 2, 0), 2, 1), 2, 2)
    grid_field = smooth_phase(grid_field, target, centre)
    return (grid_field, species_after_step)


def solution(mesh):
    in_specs = (
        P("slab", "depth", None),
        P(("slab", "depth"), None),
        P(("slab", "depth")),
        P(("slab", "depth")),
        P(("slab", "depth")),
        P(("slab", "depth")),
        P(("slab", "depth"), None),
        P(),
        P(),
        P(),
    )
    out_specs = (P("slab", "depth", None), P(("slab", "depth"), None))
    return jax.shard_map(local, mesh=mesh, in_specs=in_specs, out_specs=out_specs, check_vma=False)
```

profile of v0, /device:TPU:32, one launch (start us, length us, event | category | flops | bytes accessed | tf_op | source)
XLA Modules:
  0.0 268.3 jit_solution(16914211861482654796)
XLA Ops:
  0.7 2.1 collective-permute-start.12
  2.8 16.2 %collective-permute-start.13 = (bf16[1,16,256]{2,1,0:T(8,128)(2,1)S(1)}, bf16[1,16,256]{2,1,0:T(8,128)(2,1)S(1)}, u32[]{:S(2)}, u32[]{:S(2)}) collective-permute-start(bf16[1,16,256]{2,1,0:T(8,128)(2,1)S(1)} %broadcast.118), channel_id=1, source_target_pairs={{8,0},{16,8},{24,16},{32,24},{40,32},{48,40},{56,48},{64,56},{72,6... | collective-permute-start | bytes 24584 | tf_op jit(solution)/shard_map/ppermute | solution.py:25
  19.0 2.6 collective-permute-start.14
  21.6 4.5 %collective-permute-start.15 = (bf16[4,1,256]{2,1,0:T(2,128)(2,1)S(1)}, bf16[4,1,256]{2,1,0:T(2,128)(2,1)S(1)}, u32[]{:S(2)}, u32[]{:S(2)}) collective-permute-start(bf16[4,1,256]{2,1,0:T(2,128)(2,1)S(1)} %broadcast.120), channel_id=1, source_target_pairs={{1,0},{2,1},{3,2},{4,3},{5,4},{6,5},{7,6},{9,8},{10,9},{11,10},{12... | collective-permute-start | bytes 6152 | tf_op jit(solution)/shard_map/ppermute | solution.py:25
  26.1 1.1 convert_element_type.138
  27.2 1.9 collective-permute-start
  29.1 0.7 broadcast_clamp_fusion
  30.0 2.3 reduce-window.24
  33.1 6.2 %gather_fusion = f32[1024]{0:T(1024)S(1)} fusion(f32[131072]{0:T(1024)S(1)} %bitcast.45, s32[1024]{0:T(1024)S(1)} %get-tuple-element.60), kind=kCustom, calls=%fused_computation | custom fusion | bytes 12288 | tf_op jit(solution)/shard_map/gather | solution.py:84
  39.9 4.6 %scatter_custom_fusion.3 = bf16[2048,128]{1,0:T(8,128)(2,1)} fusion(s32[1024]{0:T(1024)S(1)} %broadcast_select_fusion, bf16[]{:T(256)} %constant.67.clone.1, bf16[1024,128]{1,0:T(8,128)(2,1)S(1)} %fusion.3, pred[1024]{0:T(1024)(128)(4,1)S(1)} %get-tuple-element.55), kind=kCustom, calls=%fused_computation.75 | custom fusion | flops 131072 | bytes 788480
  44.4 7.2 %all-to-all-start = ((bf16[8,256,128]{2,1,0:T(8,128)(2,1)}), bf16[8,256,128]{2,1,0:T(8,128)(2,1)}, u32[]{:S(2)}, u32[]{:S(2)}) async-start(bf16[8,256,128]{2,1,0:T(8,128)(2,1)} %bitcast.8), calls=%async_computation | async-start | bytes 1048576 | tf_op jit(solution)/shard_map/all_to_all | solution.py:111
  52.8 6.1 %scatter_custom_fusion = f32[131072]{0:T(1024)S(1)} fusion(s32[1024]{0:T(1024)S(1)} %get-tuple-element.61, f32[1024]{0:T(1024)S(1)} %get-tuple-element.59, f32[]{:T(128)} %constant.28.clone.1), kind=kCustom, calls=%fused_computation.78 | custom fusion | flops 1024 | bytes 524292 | tf_op jit(solution)/shard_map/scatter-add | solution.py:94
  59.0 3.1 %scatter_custom_fusion.1 = bf16[128,128]{1,0:T(8,128)(2,1)S(1)} fusion(s32[1024]{0:T(1024)S(1)} %compare_select_fusion.3, bf16[1024,128]{1,0:T(8,128)(2,1)S(1)} %fusion.3, bf16[]{:T(256)} %constant.67.clone.1), kind=kCustom, calls=%fused_computation.146 | custom fusion | bytes 32770 | tf_op jit(solution)/shard_map/scatter | solution.py:118
  62.1 3.1 %scatter_custom_fusion.2 = bf16[128,128]{1,0:T(8,128)(2,1)S(1)} fusion(s32[1024]{0:T(1024)S(1)} %compare_select_fusion.2, bf16[1024,128]{1,0:T(8,128)(2,1)S(1)} %fusion.3, bf16[]{:T(256)} %constant.67.clone.1), kind=kCustom, calls=%fused_computation.144 | custom fusion | bytes 32770 | tf_op jit(solution)/shard_map/scatter | solution.py:118
  65.3 2.5 collective-permute-start.2
  67.8 4.6 %collective-permute-start.3 = (bf16[8,1,512]{2,1,0:T(2,128)(2,1)S(1)}, bf16[8,1,512]{2,1,0:T(2,128)(2,1)S(1)}, u32[]{:S(2)}, u32[]{:S(2)}) collective-permute-start(bf16[8,1,512]{2,1,0:T(2,128)(2,1)S(1)} %get-tuple-element.41), channel_id=1, source_target_pairs={{1,0},{2,1},{3,2},{4,3},{5,4},{6,5},{7,6},{9,8},{10,9},{11,10},{12... | collective-permute-start | bytes 24584 | tf_op jit(solution)/shard_map/ppermute | solution.py:25
  72.4 5.8 %collective-permute-start.1 = (bf16[1,32,512]{2,1,0:T(8,128)(2,1)S(1)}, bf16[1,32,512]{2,1,0:T(8,128)(2,1)S(1)}, u32[]{:S(2)}, u32[]{:S(2)}) collective-permute-start(bf16[1,32,512]{2,1,0:T(8,128)(2,1)S(1)} %get-tuple-element.39), channel_id=1, source_target_pairs={{8,0},{16,8},{24,16},{32,24},{40,32},{48,40},{56,48},{64,56},{72,6... | collective-permute-start | bytes 98312 | tf_op jit(solution)/shard_map/ppermute | solution.py:25
  78.3 1.9 collective-permute-start.36
  80.3 7.0 %collective-permute-start.37 = (bf16[128,128]{1,0:T(8,128)(2,1)S(1)}, bf16[128,128]{1,0:T(8,128)(2,1)S(1)}, u32[]{:S(2)}, u32[]{:S(2)}) collective-permute-start(bf16[128,128]{1,0:T(8,128)(2,1)S(1)} %scatter_custom_fusion.2), channel_id=1, source_target_pairs={{0,760},{8,0},{16,8},{24,16},{32,24},{40,32},{48,40},{56,48},{64,5... | collective-permute-start | bytes 98312 | tf_op jit(solution)/shard_map/ppermute | solution.py:32
  88.0 1.9 collective-permute-start.6
  90.0 5.1 %collective-permute-start.7 = (bf16[8,1,512]{2,1,0:T(2,128)(2,1)S(1)}, bf16[8,1,512]{2,1,0:T(2,128)(2,1)S(1)}, u32[]{:S(2)}, u32[]{:S(2)}) collective-permute-start(bf16[8,1,512]{2,1,0:T(2,128)(2,1)S(1)} %get-tuple-element.37), channel_id=1, source_target_pairs={{1,0},{2,1},{3,2},{4,3},{5,4},{6,5},{7,6},{9,8},{10,9},{11,10},{12... | collective-permute-start | bytes 24584 | tf_op jit(solution)/shard_map/ppermute | solution.py:25
  95.1 1.9 collective-permute-start.4
  97.1 7.0 %collective-permute-start.5 = (bf16[1,32,512]{2,1,0:T(8,128)(2,1)S(1)}, bf16[1,32,512]{2,1,0:T(8,128)(2,1)S(1)}, u32[]{:S(2)}, u32[]{:S(2)}) collective-permute-start(bf16[1,32,512]{2,1,0:T(8,128)(2,1)S(1)} %get-tuple-element.35), channel_id=1, source_target_pairs={{8,0},{16,8},{24,16},{32,24},{40,32},{48,40},{56,48},{64,56},{72,6... | collective-permute-start | bytes 98312 | tf_op jit(solution)/shard_map/ppermute | solution.py:25
  104.2 1.4 collective-permute-done.5
  105.7 0.6 fusion.85
  106.3 1.9 collective-permute-start.10
  108.2 5.1 %collective-permute-start.11 = (bf16[8,1,512]{2,1,0:T(2,128)(2,1)S(1)}, bf16[8,1,512]{2,1,0:T(2,128)(2,1)S(1)}, u32[]{:S(2)}, u32[]{:S(2)}) collective-permute-start(bf16[8,1,512]{2,1,0:T(2,128)(2,1)S(1)} %get-tuple-element.33), channel_id=1, source_target_pairs={{1,0},{2,1},{3,2},{4,3},{5,4},{6,5},{7,6},{9,8},{10,9},{11,10},{12... | collective-permute-start | bytes 24584 | tf_op jit(solution)/shard_map/ppermute | solution.py:25
  113.4 1.9 collective-permute-start.8
  115.3 7.1 %collective-permute-start.9 = (bf16[1,32,512]{2,1,0:T(8,128)(2,1)S(1)}, bf16[1,32,512]{2,1,0:T(8,128)(2,1)S(1)}, u32[]{:S(2)}, u32[]{:S(2)}) collective-permute-start(bf16[1,32,512]{2,1,0:T(8,128)(2,1)S(1)} %get-tuple-element.31), channel_id=1, source_target_pairs={{8,0},{16,8},{24,16},{32,24},{40,32},{48,40},{56,48},{64,56},{72,6... | collective-permute-start | bytes 98312 | tf_op jit(solution)/shard_map/ppermute | solution.py:25
  122.6 1.3 collective-permute-done.9
  124.4 34.8 %reshape.91 = f32[4,2,16,2,256,2]{5,4,3,2,1,0:T(8,128)} reshape(f32[8,32,512]{2,1,0:T(8,128)S(1)} %fusion.19) | data formatting | bytes 1048576 | tf_op jit(solution)/shard_map/reshape | solution.py:131
  159.2 12.2 %reduce_sum.20 = f32[4,16,256]{2,1,0:T(8,128)S(1)} reduce(f32[4,2,16,2,256,2]{5,4,3,2,1,0:T(8,128)} %reshape.91, f32[]{:T(128)} %constant.28.clone.1), dimensions={1,3,5}, to_apply=%region_1.2 | reduce | flops 114688 | bytes 589828 | tf_op jit(solution)/shard_map/reduce_sum | solution.py:133
  171.6 1.9 collective-permute-start.16
  173.6 1.9 collective-permute-start.18
  175.5 5.1 %collective-permute-start.19 = (bf16[4,1,256]{2,1,0:T(2,128)(2,1)S(1)}, bf16[4,1,256]{2,1,0:T(2,128)(2,1)S(1)}, u32[]{:S(2)}, u32[]{:S(2)}) collective-permute-start(bf16[4,1,256]{2,1,0:T(2,128)(2,1)S(1)} %get-tuple-element.53), channel_id=1, source_target_pairs={{1,0},{2,1},{3,2},{4,3},{5,4},{6,5},{7,6},{9,8},{10,9},{11,10},{12... | collective-permute-start | bytes 6152 | tf_op jit(solution)/shard_map/ppermute | solution.py:25
  180.7 6.4 %collective-permute-start.17 = (bf16[1,16,256]{2,1,0:T(8,128)(2,1)S(1)}, bf16[1,16,256]{2,1,0:T(8,128)(2,1)S(1)}, u32[]{:S(2)}, u32[]{:S(2)}) collective-permute-start(bf16[1,16,256]{2,1,0:T(8,128)(2,1)S(1)} %get-tuple-element.51), channel_id=1, source_target_pairs={{8,0},{16,8},{24,16},{32,24},{40,32},{48,40},{56,48},{64,56},{72,6... | collective-permute-start | bytes 24584 | tf_op jit(solution)/shard_map/ppermute | solution.py:25
  187.1 1.3 collective-permute-done.17
  188.6 1.9 collective-permute-start.22
  190.5 5.1 %collective-permute-start.23 = (bf16[4,1,256]{2,1,0:T(2,128)(2,1)S(1)}, bf16[4,1,256]{2,1,0:T(2,128)(2,1)S(1)}, u32[]{:S(2)}, u32[]{:S(2)}) collective-permute-start(bf16[4,1,256]{2,1,0:T(2,128)(2,1)S(1)} %get-tuple-element.49), channel_id=1, source_target_pairs={{1,0},{2,1},{3,2},{4,3},{5,4},{6,5},{7,6},{9,8},{10,9},{11,10},{12... | collective-permute-start | bytes 6152 | tf_op jit(solution)/shard_map/ppermute | solution.py:25
  195.7 1.9 collective-permute-start.20
  197.6 7.0 %collective-permute-start.21 = (bf16[1,16,256]{2,1,0:T(8,128)(2,1)S(1)}, bf16[1,16,256]{2,1,0:T(8,128)(2,1)S(1)}, u32[]{:S(2)}, u32[]{:S(2)}) collective-permute-start(bf16[1,16,256]{2,1,0:T(8,128)(2,1)S(1)} %get-tuple-element.47), channel_id=1, source_target_pairs={{8,0},{16,8},{24,16},{32,24},{40,32},{48,40},{56,48},{64,56},{72,6... | collective-permute-start | bytes 24584 | tf_op jit(solution)/shard_map/ppermute | solution.py:25
  204.6 1.3 collective-permute-done.21
  206.1 1.9 collective-permute-start.26
  208.0 5.1 %collective-permute-start.27 = (bf16[4,1,256]{2,1,0:T(2,128)(2,1)S(1)}, bf16[4,1,256]{2,1,0:T(2,128)(2,1)S(1)}, u32[]{:S(2)}, u32[]{:S(2)}) collective-permute-start(bf16[4,1,256]{2,1,0:T(2,128)(2,1)S(1)} %get-tuple-element.45), channel_id=1, source_target_pairs={{1,0},{2,1},{3,2},{4,3},{5,4},{6,5},{7,6},{9,8},{10,9},{11,10},{12... | collective-permute-start | bytes 6152 | tf_op jit(solution)/shard_map/ppermute | solution.py:25
  213.1 1.9 collective-permute-start.24
  215.1 7.0 %collective-permute-start.25 = (bf16[1,16,256]{2,1,0:T(8,128)(2,1)S(1)}, bf16[1,16,256]{2,1,0:T(8,128)(2,1)S(1)}, u32[]{:S(2)}, u32[]{:S(2)}) collective-permute-start(bf16[1,16,256]{2,1,0:T(8,128)(2,1)S(1)} %get-tuple-element.43), channel_id=1, source_target_pairs={{8,0},{16,8},{24,16},{32,24},{40,32},{48,40},{56,48},{64,56},{72,6... | collective-permute-start | bytes 24584 | tf_op jit(solution)/shard_map/ppermute | solution.py:25
  222.1 1.3 collective-permute-done.25
  223.8 1.4 copy.22
  225.1 1.4 broadcast_in_dim.52
  226.5 1.5 copy.23
  228.0 1.3 fusion.79
  229.3 1.9 collective-permute-start.30
  231.2 5.1 %collective-permute-start.31 = (bf16[8,1,512]{2,1,0:T(2,128)(2,1)S(1)}, bf16[8,1,512]{2,1,0:T(2,128)(2,1)S(1)}, u32[]{:S(2)}, u32[]{:S(2)}) collective-permute-start(bf16[8,1,512]{2,1,0:T(2,128)(2,1)S(1)} %get-tuple-element.29), channel_id=1, source_target_pairs={{1,0},{2,1},{3,2},{4,3},{5,4},{6,5},{7,6},{9,8},{10,9},{11,10},{12... | collective-permute-start | bytes 24584 | tf_op jit(solution)/shard_map/ppermute | solution.py:25
  236.4 1.9 collective-permute-start.28
  238.3 7.0 %collective-permute-start.29 = (bf16[1,32,512]{2,1,0:T(8,128)(2,1)S(1)}, bf16[1,32,512]{2,1,0:T(8,128)(2,1)S(1)}, u32[]{:S(2)}, u32[]{:S(2)}) collective-permute-start(bf16[1,32,512]{2,1,0:T(8,128)(2,1)S(1)} %get-tuple-element.27), channel_id=1, source_target_pairs={{8,0},{16,8},{24,16},{32,24},{40,32},{48,40},{56,48},{64,56},{72,6... | collective-permute-start | bytes 98312 | tf_op jit(solution)/shard_map/ppermute | solution.py:25
  245.4 1.4 collective-permute-done.29
  246.9 0.6 fusion.77
  247.5 1.9 collective-permute-start.34
  249.5 5.1 %collective-permute-start.35 = (bf16[8,1,512]{2,1,0:T(2,128)(2,1)S(1)}, bf16[8,1,512]{2,1,0:T(2,128)(2,1)S(1)}, u32[]{:S(2)}, u32[]{:S(2)}) collective-permute-start(bf16[8,1,512]{2,1,0:T(2,128)(2,1)S(1)} %get-tuple-element.25), channel_id=1, source_target_pairs={{1,0},{2,1},{3,2},{4,3},{5,4},{6,5},{7,6},{9,8},{10,9},{11,10},{12... | collective-permute-start | bytes 24584 | tf_op jit(solution)/shard_map/ppermute | solution.py:25
  254.6 1.9 collective-permute-start.32
  256.6 7.0 %collective-permute-start.33 = (bf16[1,32,512]{2,1,0:T(8,128)(2,1)S(1)}, bf16[1,32,512]{2,1,0:T(8,128)(2,1)S(1)}, u32[]{:S(2)}, u32[]{:S(2)}) collective-permute-start(bf16[1,32,512]{2,1,0:T(8,128)(2,1)S(1)} %get-tuple-element.23), channel_id=1, source_target_pairs={{8,0},{16,8},{24,16},{32,24},{40,32},{48,40},{56,48},{64,56},{72,6... | collective-permute-start | bytes 98312 | tf_op jit(solution)/shard_map/ppermute | solution.py:25
  263.7 1.4 collective-permute-done.33
  265.2 1.2 fusion.31
  266.4 1.9 pad_maximum_fusion
  (131 shorter events, 5.7 us)
Async XLA Ops:
  0.6 38.9 %copy-start = (bf16[128,128]{1,0:T(8,128)(2,1)S(1)}, bf16[128,128]{1,0:T(8,128)(2,1)}, u32[]{:S(2)}) copy-start(bf16[128,128]{1,0:T(8,128)(2,1)} %param.17) | copy-start | bytes 98308
  0.6 32.2 %copy-start.10 = (s32[2]{0:T(128)S(1)}, s32[2]{0:T(128)}, u32[]{:S(2)}) copy-start(s32[2]{0:T(128)} %constant.100) | copy-start | bytes 28
  0.7 32.3 %copy-start.9 = (s32[2]{0:T(128)S(1)}, s32[2]{0:T(128)}, u32[]{:S(2)}) copy-start(s32[2]{0:T(128)} %constant.103) | copy-start | bytes 28
  0.7 29.1 %copy-start.1 = (f32[8,32,512]{2,1,0:T(8,128)S(1)}, f32[8,32,512]{2,1,0:T(8,128)}, u32[]{:S(2)}) copy-start(f32[8,32,512]{2,1,0:T(8,128)} %param.10) | copy-start | bytes 1572868
  0.7 29.3 %copy-start.4 = (s32[1024,1]{0,1:T(1,128)S(1)}, s32[1024,1]{0,1:T(1,128)}, u32[]{:S(2)}) copy-start(s32[1024,1]{0,1:T(1,128)} %param.16) | copy-start | bytes 12292
  0.7 32.3 %copy-start.5 = (s32[1024]{0:T(1024)S(1)}, s32[1024]{0:T(1024)}, u32[]{:S(2)}) copy-start(s32[1024]{0:T(1024)} %param.13) | copy-start | bytes 12292
  0.7 32.3 %copy-start.6 = (s32[1024]{0:T(1024)S(1)}, s32[1024]{0:T(1024)}, u32[]{:S(2)}) copy-start(s32[1024]{0:T(1024)} %param.15) | copy-start | bytes 12292
  0.7 79.6 %collective-permute-start.12 = (bf16[1,16,256]{2,1,0:T(8,128)(2,1)S(1)}, bf16[1,16,256]{2,1,0:T(8,128)(2,1)S(1)}, u32[]{:S(2)}, u32[]{:S(2)}) collective-permute-start(bf16[1,16,256]{2,1,0:T(8,128)(2,1)S(1)} %broadcast.118), channel_id=1, source_target_pairs={{0,8},{8,16},{16,24},{24,32},{32,40},{40,48},{48,56},{56,64},{64,7... | collective-permute-start | bytes 24584 | tf_op jit(solution)/shard_map/ppermute | solution.py:22
  2.8 84.5 %collective-permute-start.13 = (bf16[1,16,256]{2,1,0:T(8,128)(2,1)S(1)}, bf16[1,16,256]{2,1,0:T(8,128)(2,1)S(1)}, u32[]{:S(2)}, u32[]{:S(2)}) collective-permute-start(bf16[1,16,256]{2,1,0:T(8,128)(2,1)S(1)} %broadcast.118), channel_id=1, source_target_pairs={{8,0},{16,8},{24,16},{32,24},{40,32},{48,40},{56,48},{64,56},{72,6... | collective-permute-start | bytes 24584 | tf_op jit(solution)/shard_map/ppermute | solution.py:25
  19.0 46.3 %collective-permute-start.14 = (bf16[4,1,256]{2,1,0:T(2,128)(2,1)S(1)}, bf16[4,1,256]{2,1,0:T(2,128)(2,1)S(1)}, u32[]{:S(2)}, u32[]{:S(2)}) collective-permute-start(bf16[4,1,256]{2,1,0:T(2,128)(2,1)S(1)} %broadcast.120), channel_id=1, source_target_pairs={{0,1},{1,2},{2,3},{3,4},{4,5},{5,6},{6,7},{8,9},{9,10},{10,11},{11... | collective-permute-start | bytes 6152 | tf_op jit(solution)/shard_map/ppermute | solution.py:22
  21.6 46.2 %collective-permute-start.15 = (bf16[4,1,256]{2,1,0:T(2,128)(2,1)S(1)}, bf16[4,1,256]{2,1,0:T(2,128)(2,1)S(1)}, u32[]{:S(2)}, u32[]{:S(2)}) collective-permute-start(bf16[4,1,256]{2,1,0:T(2,128)(2,1)S(1)} %broadcast.120), channel_id=1, source_target_pairs={{1,0},{2,1},{3,2},{4,3},{5,4},{6,5},{7,6},{9,8},{10,9},{11,10},{12... | collective-permute-start | bytes 6152 | tf_op jit(solution)/shard_map/ppermute | solution.py:25
  27.2 60.2 %collective-permute-start = (bf16[1,32,512]{2,1,0:T(8,128)(2,1)S(1)}, bf16[1,32,512]{2,1,0:T(8,128)(2,1)S(1)}, u32[]{:S(2)}, u32[]{:S(2)}) collective-permute-start(bf16[1,32,512]{2,1,0:T(8,128)(2,1)S(1)} %get-tuple-element.38), channel_id=1, source_target_pairs={{0,8},{8,16},{16,24},{24,32},{32,40},{40,48},{48,56},{56,64},{64,7... | collective-permute-start | bytes 98312 | tf_op jit(solution)/shard_map/ppermute | solution.py:22
  33.1 6.2 %copy-start.3 = (bf16[1024,128]{1,0:T(8,128)(2,1)S(1)}, bf16[1024,128]{1,0:T(8,128)(2,1)}, u32[]{:S(2)}) copy-start(bf16[1024,128]{1,0:T(8,128)(2,1)} %param.11) | copy-start | bytes 786436
  33.1 6.2 %copy-start.8 = (bf16[128]{0:T(256)(128)(2,1)S(1)}, bf16[128]{0:T(256)(128)(2,1)}, u32[]{:S(2)}) copy-start(bf16[128]{0:T(256)(128)(2,1)} %param.19) | copy-start | bytes 772
  33.1 6.4 %copy-start.7 = (s32[1024]{0:T(1024)S(1)}, s32[1024]{0:T(1024)}, u32[]{:S(2)}) copy-start(s32[1024]{0:T(1024)} %param.14) | copy-start | bytes 12292
  33.1 6.4 %copy-start.11 = (f32[128]{0:T(128)S(1)}, f32[128]{0:T(128)}, u32[]{:S(2)}) copy-start(f32[128]{0:T(128)} %param.18) | copy-start | bytes 1540
  44.4 222.0 %all-to-all-start = ((bf16[8,256,128]{2,1,0:T(8,128)(2,1)}), bf16[8,256,128]{2,1,0:T(8,128)(2,1)}, u32[]{:S(2)}, u32[]{:S(2)}) async-start(bf16[8,256,128]{2,1,0:T(8,128)(2,1)} %bitcast.8), calls=%async_computation | async-start | bytes 1048576 | tf_op jit(solution)/shard_map/all_to_all | solution.py:111
  65.3 7.1 %collective-permute-start.2 = (bf16[8,1,512]{2,1,0:T(2,128)(2,1)S(1)}, bf16[8,1,512]{2,1,0:T(2,128)(2,1)S(1)}, u32[]{:S(2)}, u32[]{:S(2)}) collective-permute-start(bf16[8,1,512]{2,1,0:T(2,128)(2,1)S(1)} %get-tuple-element.40), channel_id=1, source_target_pairs={{0,1},{1,2},{2,3},{3,4},{4,5},{5,6},{6,7},{8,9},{9,10},{10,11},{11... | collective-permute-start | bytes 24584 | tf_op jit(solution)/shard_map/ppermute | solution.py:22
  67.8 10.5 %collective-permute-start.3 = (bf16[8,1,512]{2,1,0:T(2,128)(2,1)S(1)}, bf16[8,1,512]{2,1,0:T(2,128)(2,1)S(1)}, u32[]{:S(2)}, u32[]{:S(2)}) collective-permute-start(bf16[8,1,512]{2,1,0:T(2,128)(2,1)S(1)} %get-tuple-element.41), channel_id=1, source_target_pairs={{1,0},{2,1},{3,2},{4,3},{5,4},{6,5},{7,6},{9,8},{10,9},{11,10},{12... | collective-permute-start | bytes 24584 | tf_op jit(solution)/shard_map/ppermute | solution.py:25
  72.4 14.9 %collective-permute-start.1 = (bf16[1,32,512]{2,1,0:T(8,128)(2,1)S(1)}, bf16[1,32,512]{2,1,0:T(8,128)(2,1)S(1)}, u32[]{:S(2)}, u32[]{:S(2)}) collective-permute-start(bf16[1,32,512]{2,1,0:T(8,128)(2,1)S(1)} %get-tuple-element.39), channel_id=1, source_target_pairs={{8,0},{16,8},{24,16},{32,24},{40,32},{48,40},{56,48},{64,56},{72,6... | collective-permute-start | bytes 98312 | tf_op jit(solution)/shard_map/ppermute | solution.py:25
  78.3 188.1 %collective-permute-start.36 = (bf16[128,128]{1,0:T(8,128)(2,1)S(1)}, bf16[128,128]{1,0:T(8,128)(2,1)S(1)}, u32[]{:S(2)}, u32[]{:S(2)}) collective-permute-start(bf16[128,128]{1,0:T(8,128)(2,1)S(1)} %scatter_custom_fusion.1), channel_id=1, source_target_pairs={{0,8},{8,16},{16,24},{24,32},{32,40},{40,48},{48,56},{56,64},{64,7... | collective-permute-start | bytes 98312 | tf_op jit(solution)/shard_map/ppermute | solution.py:32
  80.3 186.1 %collective-permute-start.37 = (bf16[128,128]{1,0:T(8,128)(2,1)S(1)}, bf16[128,128]{1,0:T(8,128)(2,1)S(1)}, u32[]{:S(2)}, u32[]{:S(2)}) collective-permute-start(bf16[128,128]{1,0:T(8,128)(2,1)S(1)} %scatter_custom_fusion.2), channel_id=1, source_target_pairs={{0,760},{8,0},{16,8},{24,16},{32,24},{40,32},{48,40},{56,48},{64,5... | collective-permute-start | bytes 98312 | tf_op jit(solution)/shard_map/ppermute | solution.py:32
  88.0 9.0 %collective-permute-start.6 = (bf16[8,1,512]{2,1,0:T(2,128)(2,1)S(1)}, bf16[8,1,512]{2,1,0:T(2,128)(2,1)S(1)}, u32[]{:S(2)}, u32[]{:S(2)}) collective-permute-start(bf16[8,1,512]{2,1,0:T(2,128)(2,1)S(1)} %get-tuple-element.36), channel_id=1, source_target_pairs={{0,1},{1,2},{2,3},{3,4},{4,5},{5,6},{6,7},{8,9},{9,10},{10,11},{11... | collective-permute-start | bytes 24584 | tf_op jit(solution)/shard_map/ppermute | solution.py:22
  90.0 14.1 %collective-permute-start.7 = (bf16[8,1,512]{2,1,0:T(2,128)(2,1)S(1)}, bf16[8,1,512]{2,1,0:T(2,128)(2,1)S(1)}, u32[]{:S(2)}, u32[]{:S(2)}) collective-permute-start(bf16[8,1,512]{2,1,0:T(2,128)(2,1)S(1)} %get-tuple-element.37), channel_id=1, source_target_pairs={{1,0},{2,1},{3,2},{4,3},{5,4},{6,5},{7,6},{9,8},{10,9},{11,10},{12... | collective-permute-start | bytes 24584 | tf_op jit(solution)/shard_map/ppermute | solution.py:25
  95.1 9.0 %collective-permute-start.4 = (bf16[1,32,512]{2,1,0:T(8,128)(2,1)S(1)}, bf16[1,32,512]{2,1,0:T(8,128)(2,1)S(1)}, u32[]{:S(2)}, u32[]{:S(2)}) collective-permute-start(bf16[1,32,512]{2,1,0:T(8,128)(2,1)S(1)} %get-tuple-element.34), channel_id=1, source_target_pairs={{0,8},{8,16},{16,24},{24,32},{32,40},{40,48},{48,56},{56,64},{64,7... | collective-permute-start | bytes 98312 | tf_op jit(solution)/shard_map/ppermute | solution.py:22
  97.1 8.5 %collective-permute-start.5 = (bf16[1,32,512]{2,1,0:T(8,128)(2,1)S(1)}, bf16[1,32,512]{2,1,0:T(8,128)(2,1)S(1)}, u32[]{:S(2)}, u32[]{:S(2)}) collective-permute-start(bf16[1,32,512]{2,1,0:T(8,128)(2,1)S(1)} %get-tuple-element.35), channel_id=1, source_target_pairs={{8,0},{16,8},{24,16},{32,24},{40,32},{48,40},{56,48},{64,56},{72,6... | collective-permute-start | bytes 98312 | tf_op jit(solution)/shard_map/ppermute | solution.py:25
  106.2 17.7 %copy-start.2 = (f32[8,32,512]{2,1,0:T(8,128)}, f32[8,32,512]{2,1,0:T(8,128)S(1)}, u32[]{:S(2)}) copy-start(f32[8,32,512]{2,1,0:T(8,128)S(1)} %get-tuple-element.19) | copy-start | bytes 1572868
  106.3 9.0 %collective-permute-start.10 = (bf16[8,1,512]{2,1,0:T(2,128)(2,1)S(1)}, bf16[8,1,512]{2,1,0:T(2,128)(2,1)S(1)}, u32[]{:S(2)}, u32[]{:S(2)}) collective-permute-start(bf16[8,1,512]{2,1,0:T(2,128)(2,1)S(1)} %get-tuple-element.32), channel_id=1, source_target_pairs={{0,1},{1,2},{2,3},{3,4},{4,5},{5,6},{6,7},{8,9},{9,10},{10,11},{11... | collective-permute-start | bytes 24584 | tf_op jit(solution)/shard_map/ppermute | solution.py:22
  108.2 14.2 %collective-permute-start.11 = (bf16[8,1,512]{2,1,0:T(2,128)(2,1)S(1)}, bf16[8,1,512]{2,1,0:T(2,128)(2,1)S(1)}, u32[]{:S(2)}, u32[]{:S(2)}) collective-permute-start(bf16[8,1,512]{2,1,0:T(2,128)(2,1)S(1)} %get-tuple-element.33), channel_id=1, source_target_pairs={{1,0},{2,1},{3,2},{4,3},{5,4},{6,5},{7,6},{9,8},{10,9},{11,10},{12... | collective-permute-start | bytes 24584 | tf_op jit(solution)/shard_map/ppermute | solution.py:25
  113.4 9.2 %collective-permute-start.8 = (bf16[1,32,512]{2,1,0:T(8,128)(2,1)S(1)}, bf16[1,32,512]{2,1,0:T(8,128)(2,1)S(1)}, u32[]{:S(2)}, u32[]{:S(2)}) collective-permute-start(bf16[1,32,512]{2,1,0:T(8,128)(2,1)S(1)} %get-tuple-element.30), channel_id=1, source_target_pairs={{0,8},{8,16},{16,24},{24,32},{32,40},{40,48},{48,56},{56,64},{64,7... | collective-permute-start | bytes 98312 | tf_op jit(solution)/shard_map/ppermute | solution.py:22
  115.3 8.5 %collective-permute-start.9 = (bf16[1,32,512]{2,1,0:T(8,128)(2,1)S(1)}, bf16[1,32,512]{2,1,0:T(8,128)(2,1)S(1)}, u32[]{:S(2)}, u32[]{:S(2)}) collective-permute-start(bf16[1,32,512]{2,1,0:T(8,128)(2,1)S(1)} %get-tuple-element.31), channel_id=1, source_target_pairs={{8,0},{16,8},{24,16},{32,24},{40,32},{48,40},{56,48},{64,56},{72,6... | collective-permute-start | bytes 98312 | tf_op jit(solution)/shard_map/ppermute | solution.py:25
  171.6 15.5 %collective-permute-start.16 = (bf16[1,16,256]{2,1,0:T(8,128)(2,1)S(1)}, bf16[1,16,256]{2,1,0:T(8,128)(2,1)S(1)}, u32[]{:S(2)}, u32[]{:S(2)}) collective-permute-start(bf16[1,16,256]{2,1,0:T(8,128)(2,1)S(1)} %get-tuple-element.50), channel_id=1, source_target_pairs={{0,8},{8,16},{16,24},{24,32},{32,40},{40,48},{48,56},{56,64},{64,7... | collective-permute-start | bytes 24584 | tf_op jit(solution)/shard_map/ppermute | solution.py:22
  173.6 7.1 %collective-permute-start.18 = (bf16[4,1,256]{2,1,0:T(2,128)(2,1)S(1)}, bf16[4,1,256]{2,1,0:T(2,128)(2,1)S(1)}, u32[]{:S(2)}, u32[]{:S(2)}) collective-permute-start(bf16[4,1,256]{2,1,0:T(2,128)(2,1)S(1)} %get-tuple-element.52), channel_id=1, source_target_pairs={{0,1},{1,2},{2,3},{3,4},{4,5},{5,6},{6,7},{8,9},{9,10},{10,11},{11... | collective-permute-start | bytes 6152 | tf_op jit(solution)/shard_map/ppermute | solution.py:22
  175.5 11.6 %collective-permute-start.19 = (bf16[4,1,256]{2,1,0:T(2,128)(2,1)S(1)}, bf16[4,1,256]{2,1,0:T(2,128)(2,1)S(1)}, u32[]{:S(2)}, u32[]{:S(2)}) collective-permute-start(bf16[4,1,256]{2,1,0:T(2,128)(2,1)S(1)} %get-tuple-element.53), channel_id=1, source_target_pairs={{1,0},{2,1},{3,2},{4,3},{5,4},{6,5},{7,6},{9,8},{10,9},{11,10},{12... | collective-permute-start | bytes 6152 | tf_op jit(solution)/shard_map/ppermute | solution.py:25
  180.7 7.8 %collective-permute-start.17 = (bf16[1,16,256]{2,1,0:T(8,128)(2,1)S(1)}, bf16[1,16,256]{2,1,0:T(8,128)(2,1)S(1)}, u32[]{:S(2)}, u32[]{:S(2)}) collective-permute-start(bf16[1,16,256]{2,1,0:T(8,128)(2,1)S(1)} %get-tuple-element.51), channel_id=1, source_target_pairs={{8,0},{16,8},{24,16},{32,24},{40,32},{48,40},{56,48},{64,56},{72,6... | collective-permute-start | bytes 24584 | tf_op jit(solution)/shard_map/ppermute | solution.py:25
  188.6 9.0 %collective-permute-start.22 = (bf16[4,1,256]{2,1,0:T(2,128)(2,1)S(1)}, bf16[4,1,256]{2,1,0:T(2,128)(2,1)S(1)}, u32[]{:S(2)}, u32[]{:S(2)}) collective-permute-start(bf16[4,1,256]{2,1,0:T(2,128)(2,1)S(1)} %get-tuple-element.48), channel_id=1, source_target_pairs={{0,1},{1,2},{2,3},{3,4},{4,5},{5,6},{6,7},{8,9},{9,10},{10,11},{11... | collective-permute-start | bytes 6152 | tf_op jit(solution)/shard_map/ppermute | solution.py:22
  190.5 14.1 %collective-permute-start.23 = (bf16[4,1,256]{2,1,0:T(2,128)(2,1)S(1)}, bf16[4,1,256]{2,1,0:T(2,128)(2,1)S(1)}, u32[]{:S(2)}, u32[]{:S(2)}) collective-permute-start(bf16[4,1,256]{2,1,0:T(2,128)(2,1)S(1)} %get-tuple-element.49), channel_id=1, source_target_pairs={{1,0},{2,1},{3,2},{4,3},{5,4},{6,5},{7,6},{9,8},{10,9},{11,10},{12... | collective-permute-start | bytes 6152 | tf_op jit(solution)/shard_map/ppermute | solution.py:25
  195.7 9.0 %collective-permute-start.20 = (bf16[1,16,256]{2,1,0:T(8,128)(2,1)S(1)}, bf16[1,16,256]{2,1,0:T(8,128)(2,1)S(1)}, u32[]{:S(2)}, u32[]{:S(2)}) collective-permute-start(bf16[1,16,256]{2,1,0:T(8,128)(2,1)S(1)} %get-tuple-element.46), channel_id=1, source_target_pairs={{0,8},{8,16},{16,24},{24,32},{32,40},{40,48},{48,56},{56,64},{64,7... | collective-permute-start | bytes 24584 | tf_op jit(solution)/shard_map/ppermute | solution.py:22
  197.6 8.3 %collective-permute-start.21 = (bf16[1,16,256]{2,1,0:T(8,128)(2,1)S(1)}, bf16[1,16,256]{2,1,0:T(8,128)(2,1)S(1)}, u32[]{:S(2)}, u32[]{:S(2)}) collective-permute-start(bf16[1,16,256]{2,1,0:T(8,128)(2,1)S(1)} %get-tuple-element.47), channel_id=1, source_target_pairs={{8,0},{16,8},{24,16},{32,24},{40,32},{48,40},{56,48},{64,56},{72,6... | collective-permute-start | bytes 24584 | tf_op jit(solution)/shard_map/ppermute | solution.py:25
  206.1 9.0 %collective-permute-start.26 = (bf16[4,1,256]{2,1,0:T(2,128)(2,1)S(1)}, bf16[4,1,256]{2,1,0:T(2,128)(2,1)S(1)}, u32[]{:S(2)}, u32[]{:S(2)}) collective-permute-start(bf16[4,1,256]{2,1,0:T(2,128)(2,1)S(1)} %get-tuple-element.44), channel_id=1, source_target_pairs={{0,1},{1,2},{2,3},{3,4},{4,5},{5,6},{6,7},{8,9},{9,10},{10,11},{11... | collective-permute-start | bytes 6152 | tf_op jit(solution)/shard_map/ppermute | solution.py:22
  208.0 14.1 %collective-permute-start.27 = (bf16[4,1,256]{2,1,0:T(2,128)(2,1)S(1)}, bf16[4,1,256]{2,1,0:T(2,128)(2,1)S(1)}, u32[]{:S(2)}, u32[]{:S(2)}) collective-permute-start(bf16[4,1,256]{2,1,0:T(2,128)(2,1)S(1)} %get-tuple-element.45), channel_id=1, source_target_pairs={{1,0},{2,1},{3,2},{4,3},{5,4},{6,5},{7,6},{9,8},{10,9},{11,10},{12... | collective-permute-start | bytes 6152 | tf_op jit(solution)/shard_map/ppermute | solution.py:25
  213.1 9.0 %collective-permute-start.24 = (bf16[1,16,256]{2,1,0:T(8,128)(2,1)S(1)}, bf16[1,16,256]{2,1,0:T(8,128)(2,1)S(1)}, u32[]{:S(2)}, u32[]{:S(2)}) collective-permute-start(bf16[1,16,256]{2,1,0:T(8,128)(2,1)S(1)} %get-tuple-element.42), channel_id=1, source_target_pairs={{0,8},{8,16},{16,24},{24,32},{32,40},{40,48},{48,56},{56,64},{64,7... | collective-permute-start | bytes 24584 | tf_op jit(solution)/shard_map/ppermute | solution.py:22
  215.1 8.3 %collective-permute-start.25 = (bf16[1,16,256]{2,1,0:T(8,128)(2,1)S(1)}, bf16[1,16,256]{2,1,0:T(8,128)(2,1)S(1)}, u32[]{:S(2)}, u32[]{:S(2)}) collective-permute-start(bf16[1,16,256]{2,1,0:T(8,128)(2,1)S(1)} %get-tuple-element.43), channel_id=1, source_target_pairs={{8,0},{16,8},{24,16},{32,24},{40,32},{48,40},{56,48},{64,56},{72,6... | collective-permute-start | bytes 24584 | tf_op jit(solution)/shard_map/ppermute | solution.py:25
  229.3 9.0 %collective-permute-start.30 = (bf16[8,1,512]{2,1,0:T(2,128)(2,1)S(1)}, bf16[8,1,512]{2,1,0:T(2,128)(2,1)S(1)}, u32[]{:S(2)}, u32[]{:S(2)}) collective-permute-start(bf16[8,1,512]{2,1,0:T(2,128)(2,1)S(1)} %get-tuple-element.28), channel_id=1, source_target_pairs={{0,1},{1,2},{2,3},{3,4},{4,5},{5,6},{6,7},{8,9},{9,10},{10,11},{11... | collective-permute-start | bytes 24584 | tf_op jit(solution)/shard_map/ppermute | solution.py:22
  231.2 14.1 %collective-permute-start.31 = (bf16[8,1,512]{2,1,0:T(2,128)(2,1)S(1)}, bf16[8,1,512]{2,1,0:T(2,128)(2,1)S(1)}, u32[]{:S(2)}, u32[]{:S(2)}) collective-permute-start(bf16[8,1,512]{2,1,0:T(2,128)(2,1)S(1)} %get-tuple-element.29), channel_id=1, source_target_pairs={{1,0},{2,1},{3,2},{4,3},{5,4},{6,5},{7,6},{9,8},{10,9},{11,10},{12... | collective-permute-start | bytes 24584 | tf_op jit(solution)/shard_map/ppermute | solution.py:25
  236.4 9.0 %collective-permute-start.28 = (bf16[1,32,512]{2,1,0:T(8,128)(2,1)S(1)}, bf16[1,32,512]{2,1,0:T(8,128)(2,1)S(1)}, u32[]{:S(2)}, u32[]{:S(2)}) collective-permute-start(bf16[1,32,512]{2,1,0:T(8,128)(2,1)S(1)} %get-tuple-element.26), channel_id=1, source_target_pairs={{0,8},{8,16},{16,24},{24,32},{32,40},{40,48},{48,56},{56,64},{64,7... | collective-permute-start | bytes 98312 | tf_op jit(solution)/shard_map/ppermute | solution.py:22
  238.3 8.5 %collective-permute-start.29 = (bf16[1,32,512]{2,1,0:T(8,128)(2,1)S(1)}, bf16[1,32,512]{2,1,0:T(8,128)(2,1)S(1)}, u32[]{:S(2)}, u32[]{:S(2)}) collective-permute-start(bf16[1,32,512]{2,1,0:T(8,128)(2,1)S(1)} %get-tuple-element.27), channel_id=1, source_target_pairs={{8,0},{16,8},{24,16},{32,24},{40,32},{48,40},{56,48},{64,56},{72,6... | collective-permute-start | bytes 98312 | tf_op jit(solution)/shard_map/ppermute | solution.py:25
  247.5 9.0 %collective-permute-start.34 = (bf16[8,1,512]{2,1,0:T(2,128)(2,1)S(1)}, bf16[8,1,512]{2,1,0:T(2,128)(2,1)S(1)}, u32[]{:S(2)}, u32[]{:S(2)}) collective-permute-start(bf16[8,1,512]{2,1,0:T(2,128)(2,1)S(1)} %get-tuple-element.24), channel_id=1, source_target_pairs={{0,1},{1,2},{2,3},{3,4},{4,5},{5,6},{6,7},{8,9},{9,10},{10,11},{11... | collective-permute-start | bytes 24584 | tf_op jit(solution)/shard_map/ppermute | solution.py:22
  249.5 14.1 %collective-permute-start.35 = (bf16[8,1,512]{2,1,0:T(2,128)(2,1)S(1)}, bf16[8,1,512]{2,1,0:T(2,128)(2,1)S(1)}, u32[]{:S(2)}, u32[]{:S(2)}) collective-permute-start(bf16[8,1,512]{2,1,0:T(2,128)(2,1)S(1)} %get-tuple-element.25), channel_id=1, source_target_pairs={{1,0},{2,1},{3,2},{4,3},{5,4},{6,5},{7,6},{9,8},{10,9},{11,10},{12... | collective-permute-start | bytes 24584 | tf_op jit(solution)/shard_map/ppermute | solution.py:25
  254.6 9.0 %collective-permute-start.32 = (bf16[1,32,512]{2,1,0:T(8,128)(2,1)S(1)}, bf16[1,32,512]{2,1,0:T(8,128)(2,1)S(1)}, u32[]{:S(2)}, u32[]{:S(2)}) collective-permute-start(bf16[1,32,512]{2,1,0:T(8,128)(2,1)S(1)} %get-tuple-element.22), channel_id=1, source_target_pairs={{0,8},{8,16},{16,24},{24,32},{32,40},{40,48},{48,56},{56,64},{64,7... | collective-permute-start | bytes 98312 | tf_op jit(solution)/shard_map/ppermute | solution.py:22
  256.6 8.5 %collective-permute-start.33 = (bf16[1,32,512]{2,1,0:T(8,128)(2,1)S(1)}, bf16[1,32,512]{2,1,0:T(8,128)(2,1)S(1)}, u32[]{:S(2)}, u32[]{:S(2)}) collective-permute-start(bf16[1,32,512]{2,1,0:T(8,128)(2,1)S(1)} %get-tuple-element.23), channel_id=1, source_target_pairs={{8,0},{16,8},{24,16},{32,24},{40,32},{48,40},{56,48},{64,56},{72,6... | collective-permute-start | bytes 98312 | tf_op jit(solution)/shard_map/ppermute | solution.py:25
where the time goes:
time: 270 us; the launch traced here: 268 us
  starting transfers between devices  167 us (62%)
  local copies, waits for them, and re-layouts  52.9 us (20%)
  other arithmetic  36.1 us (13%)
  waiting for transfers between devices  9.53 us (4%)
    ppermute x18, starting transfers between devices, extended(): lax.ppermute(lax.slice_in_dim(block, 0, width, axis=dim), axis, backward)  115 us
    ppermute x18, starting transfers between devices, extended(): lax.ppermute(lax.slice_in_dim(block, block.shape[dim] - width, None, axis...  35.9 us
    reshape x1, local copies, waits for them, and re-layouts, local(): residual.reshape(first_cells // 2, 2, second_cells // 2, 2, third_cells /...  34.8 us
    reduce_sum x1, other arithmetic, local(): coarse_target = 4.0 * residual.reshape(first_cells // 2, 2, second_cells...  12.2 us
    ppermute x18, waiting for transfers between devices, extended(): lax.ppermute(lax.slice_in_dim(block, 0, width, axis=dim), axis, backward)  9.48 us
    ppermute x2, starting transfers between devices, passed_along(): lax.ppermute(array, axis, [(i, (i + by) % count) for i in range(count)])  8.88 us
    all_to_all x1, starting transfers between devices, local(): lax.all_to_all(packed, 'depth', split_axis=0, concat_axis=0, tiled=True)  7.21 us
    scatter x2, local copies, waits for them, and re-layouts, local(): outgoing.append(jnp.zeros((MIG, width), jnp.bfloat16).at[jnp.where(chosen...  6.29 us
  transfers between devices with their start and end apart: 39, of which 7 were waited for; matrix products, arithmetic and copies ran while one was open for 33% of the time, Pallas kernels for 0%

commit v1 on v0

v1 whole, which is shorter than its diff:
```python
import functools

import jax
import jax.numpy as jnp
from jax import lax
from jax.experimental import pallas as pl
from jax.experimental.pallas import tpu as pltpu
from jax.sharding import PartitionSpec as P

SCREENING = 0.05
DAMPING = 2.0 / 3.0
CENTRE = 6.0 + SCREENING
COARSE_CENTRE = 6.0 + 4.0 * SCREENING
F32 = jnp.float32
BF16 = jnp.bfloat16
I32 = jnp.int32
MESH = pl.DeviceIdType.MESH
HIGHEST = lax.Precision.HIGHEST

ROWS = 1024
CAP = 256
MIG = 128
WIDTH = 128
SIDES = ((1, 0), (-1, 0), (0, 1), (0, -1), (1, 1), (1, -1), (-1, 1), (-1, -1))


def iota(shape, axis, dtype=I32):
    values = lax.broadcasted_iota(I32, shape, axis)
    return values if dtype == I32 else values.astype(dtype)


def neighbour_sum(centre, below, above, first_lane, last_lane):
    rows, lanes = centre.shape
    left = jnp.where(first_lane, 0.0, pltpu.roll(centre, 1, 1))
    right = jnp.where(last_lane, 0.0, pltpu.roll(centre, lanes - 1, 1))
    low = pltpu.roll(centre, 1, 0)
    high = pltpu.roll(centre, rows - 1, 0)
    return (below + above) + (low + high) + (left + right)


def kernel(
    n_slab, n_depth,
    nut, spec, cell, death, divide, move, route, netw, sensing, uw,
    grid_out, spec_out,
    nb, nb_low, nb_high, src, src_low, src_high, cb, cb_low, cb_high,
    xr_low, xr_high, yr_low, yr_high,
    xs_low, xs_high, ys_low, ys_high,
    xc_low, xc_high, yc_low, yc_high,
    lane_hot, upd, packed, movers, sbuf, tbuf, ubuf, vbuf, rbuf, cbuf, dbuf, ebuf,
    halo_send, halo_recv, a2a_send, a2a_recv, mig_send, mig_recv,
):
    s = lax.axis_index("slab")
    d = lax.axis_index("depth")

    def at(step_s, step_d):
        return (lax.rem(s + step_s + n_slab, n_slab), lax.rem(d + step_d + n_depth, n_depth))

    barrier = pltpu.get_barrier_semaphore()
    partners = [at(a, b) for a, b in SIDES if a != 0] + [at(0, k) for k in range(1, n_depth)]
    for partner in partners:
        pl.semaphore_signal(barrier, inc=1, device_id=partner, device_id_type=MESH)

    def exchange(number, sources, targets):
        copies = []
        for i, (a, b) in enumerate(SIDES):
            copy = pltpu.make_async_remote_copy(
                src_ref=sources[i],
                dst_ref=targets[i],
                send_sem=halo_send.at[number, i],
                recv_sem=halo_recv.at[number, i],
                device_id=at(a, b),
                device_id_type=MESH,
            )
            copy.start()
            copies.append(copy)
        return copies

    for x in range(8):
        plane = nut[x].astype(BF16)
        nb[x] = plane
        nb_low[x] = plane[0:4]
        nb_high[x] = plane[28:32]

    cell_row = cell[...]
    z_row = lax.rem(cell_row, 512)
    xy_row = lax.div(cell_row, 512)

    def fill_lane(i, carry):
        start = pl.multiple_of(i * 64, 64)
        hit = (iota((64, ROWS), 0) + start) == z_row
        lane_hot[pl.ds(start, 64), :] = jnp.where(hit, 1.0, 0.0).astype(BF16)
        return carry

    lax.fori_loop(0, 8, fill_lane, 0)
    sampled = jnp.dot(nb[...].reshape(256, 512), lane_hot[...], preferred_element_type=F32)
    row_hit = iota((256, ROWS), 0) == xy_row
    sample = jnp.sum(jnp.where(row_hit, sampled, 0.0), axis=0, keepdims=True)

    alive = 1.0 - death[...].astype(F32)
    score = lax.dot_general(
        jnp.broadcast_to(uw[...], (16, WIDTH)), spec[...], (((1,), (1,)), ((), ())),
        preferred_element_type=F32,
    )[0:1]
    softplus = jnp.maximum(score, 0.0) + jnp.log1p(jnp.exp(-jnp.abs(score)))
    uptake = alive * (1.0 + divide[...].astype(F32)) * softplus * sample / (0.5 + sample)

    pl.semaphore_wait(barrier, len(partners))
    first = exchange(
        0,
        [nb.at[pl.ds(4, 4)], nb.at[pl.ds(0, 4)], nb_high, nb_low,
         nb_high.at[pl.ds(4, 4)], nb_low.at[pl.ds(4, 4)],
         nb_high.at[pl.ds(0, 4)], nb_low.at[pl.ds(0, 4)]],
        [xr_low, xr_high, yr_low.at[pl.ds(4, 8)], yr_high.at[pl.ds(4, 8)],
         yr_low.at[pl.ds(0, 4)], yr_high.at[pl.ds(0, 4)],
         yr_low.at[pl.ds(12, 4)], yr_high.at[pl.ds(12, 4)]],
    )

    piece = uptake.astype(BF16).astype(F32)
    rest = uptake - piece
    row_hit = iota((256, ROWS), 0) == xy_row
    pieces = jnp.concatenate(
        [jnp.where(row_hit, piece, 0.0).astype(BF16), jnp.where(row_hit, rest, 0.0).astype(BF16)],
        axis=0,
    )
    sources = lax.dot_general(
        pieces, lane_hot[...], (((1,), (1,)), ((), ())), preferred_element_type=F32
    )
    source = (sources[0:256] + sources[256:512]).reshape(8, 32, 512)
    for x in range(8):
        plane = source[x]
        rounded = plane.astype(BF16)
        src[x] = rounded
        src_low[x] = rounded[0:4]
        src_high[x] = rounded[28:32]
        ubuf[4 + x, 0:32, :] = nut[x]
        tbuf[4 + x, 0:32, :] = SCREENING * nut[x] - plane
    second = exchange(
        1,
        [src.at[pl.ds(5, 3)], src.at[pl.ds(0, 3)], src_high, src_low,
         src_high.at[pl.ds(5, 3)], src_low.at[pl.ds(5, 3)],
         src_high.at[pl.ds(0, 3)], src_low.at[pl.ds(0, 3)]],
        [xs_low.at[pl.ds(1, 3)], xs_high.at[pl.ds(0, 3)],
         ys_low.at[pl.ds(4, 8)], ys_high.at[pl.ds(4, 8)],
         ys_low.at[pl.ds(1, 3)], ys_high.at[pl.ds(1, 3)],
         ys_low.at[pl.ds(12, 3)], ys_high.at[pl.ds(12, 3)]],
    )

    sensed = sample.astype(BF16).astype(F32)
    activation = jnp.dot(spec[...], netw[...], preferred_element_type=F32)
    sensed_column = jnp.transpose(jnp.broadcast_to(sensed, (WIDTH, ROWS)))
    activation = activation + sensed_column * sensing[...]
    upd[...] = (0.5 * spec[...].astype(F32) + jnp.tanh(activation)).astype(BF16)

    lanes = iota((16, ROWS), 0)
    move_row = move[...]
    route_row = route[...]
    counted = (lanes == route_row) | (lanes == 7 + move_row) & (move_row > 0)
    counted = jnp.where(counted, 1.0, 0.0)
    chosen = jnp.where(move_row == 0, route_row, 7 + move_row)
    stacked = jnp.concatenate([counted[:, a * 128:(a + 1) * 128] for a in range(8)], axis=0)
    before = jnp.where(iota((128, 128), 0) < iota((128, 128), 1), 1.0, 0.0)
    inside = jnp.dot(stacked.astype(BF16), before.astype(BF16), preferred_element_type=F32)
    total = jnp.dot(stacked.astype(BF16), jnp.ones((128, 128), BF16), preferred_element_type=F32)
    offset = jnp.zeros((16, 128), F32)
    ranks = []
    for a in range(8):
        ranks.append(inside[a * 16:(a + 1) * 16] + offset)
        offset = offset + total[a * 16:(a + 1) * 16]
    rank = jnp.concatenate(ranks, axis=1)
    rank = jnp.sum(jnp.where(lanes == chosen, rank, 0.0), axis=0, keepdims=True)
    rank = jnp.where(alive > 0.0, rank, -1.0)
    chosen = chosen.astype(F32)

    def pack(destination, slots):
        key = jnp.where(chosen == destination, rank, -1.0)
        hot = jnp.where(iota((slots, ROWS), 0, F32) == key, 1.0, 0.0).astype(BF16)
        return jnp.dot(hot, upd[...], preferred_element_type=F32).astype(BF16)

    def pack_step(k, carry):
        packed[k] = pack(lax.rem(d + k, n_depth).astype(F32), CAP)
        return carry

    lax.fori_loop(1, n_depth, pack_step, 0)
    movers[0] = pack(8.0, MIG)
    movers[1] = pack(9.0, MIG)
    own = pl.multiple_of(d * CAP, CAP)
    spec_out[pl.ds(own, CAP), :] = pack(d.astype(F32), CAP)

    def send_block(k):
        copy = pltpu.make_async_remote_copy(
            src_ref=packed.at[k],
            dst_ref=spec_out.at[pl.ds(own, CAP), :],
            send_sem=a2a_send.at[k],
            recv_sem=a2a_recv.at[k],
            device_id=at(0, k),
            device_id_type=MESH,
        )
        copy.start()
        return copy

    blocks = [send_block(k) for k in (4, 3, 5)]

    lane = iota((1, 512), 1)
    first_lane = lane == 0
    last_lane = lane == 511
    row8 = iota((8, 1), 0)
    inside_domain = ((row8 < 4) & (d < n_depth - 1)) | ((row8 >= 4) & (d > 0))
    for copy in first + second:
        copy.wait_recv()

    def halo_rows(high, low):
        joined = jnp.concatenate([high.astype(F32), low.astype(F32)], axis=0)
        return jnp.where(inside_domain, joined, 0.0)

    def outer(x, low, high, s_low, s_high, i):
        value = (low if low is not None else high)[i].astype(F32)
        ubuf[x, 0:32, :] = value
        tbuf[x, 0:32, :] = SCREENING * value - (s_low if s_low is not None else s_high)[i].astype(F32)

    for i in range(1, 4):
        outer(i, xr_low, None, xs_low, None, i)
    for i in range(0, 3):
        outer(12 + i, None, xr_high, None, xs_high, i)
    ubuf[0, 0:32, :] = xr_low[0].astype(F32)
    ubuf[15, 0:32, :] = xr_high[3].astype(F32)

    def fill_rows(x, carry):
        value = halo_rows(yr_high[x], yr_low[x])
        ubuf[x, 32:40, :] = value
        tbuf[x, 32:40, :] = SCREENING * value - halo_rows(ys_high[x], ys_low[x])
        return carry

    lax.fori_loop(0, 16, fill_rows, 0)

    def masked(value):
        rows = value.shape[0] - 8
        return jnp.concatenate([value[0:rows], jnp.where(inside_domain, value[rows:], 0.0)], axis=0)

    def sweep(source_ref, x):
        value = source_ref[x]
        around = neighbour_sum(value, source_ref[x - 1], source_ref[x + 1], first_lane, last_lane)
        return value * (1.0 - DAMPING) + (DAMPING / CENTRE) * (tbuf[x] + around)

    def sweep_first(x, carry):
        vbuf[x] = masked(sweep(ubuf, x))
        return carry

    def sweep_second(x, carry):
        ubuf[x] = masked(sweep(vbuf, x))
        return carry

    lax.fori_loop(1, 15, sweep_first, 0)
    lax.fori_loop(2, 14, sweep_second, 0)

    def residual(x, carry):
        value = ubuf[x]
        around = neighbour_sum(value, ubuf[x - 1], ubuf[x + 1], first_lane, last_lane)
        rbuf[x - 4] = tbuf[x, 0:32, :] - (CENTRE * value - around)[0:32]
        return carry

    lax.fori_loop(4, 12, residual, 0)

    planes = jnp.concatenate([rbuf[2 * p] + rbuf[2 * p + 1] for p in range(4)], axis=0)
    lane_pairs = jnp.where(lax.div(iota((512, 256), 0), 2) == iota((512, 256), 1), 1.0, 0.0)
    row_pairs = jnp.where(iota((64, 128), 0) == lax.div(iota((64, 128), 1), 2), 1.0, 0.0)
    halved = jnp.dot(planes, lane_pairs, preferred_element_type=F32, precision=HIGHEST)
    coarse_target = 0.5 * jnp.dot(row_pairs, halved, preferred_element_type=F32, precision=HIGHEST)
    for p in range(4):
        plane = coarse_target[p * 16:(p + 1) * 16]
        rounded = plane.astype(BF16)
        cb[p] = rounded
        cb_low[p] = rounded[0:4]
        cb_high[p] = rounded[12:16]
        cbuf[4 + p, 0:16, :] = plane
    third = exchange(
        2,
        [cb, cb, cb_high, cb_low, cb_high, cb_low, cb_high, cb_low],
        [xc_low, xc_high, yc_low.at[pl.ds(4, 4)], yc_high.at[pl.ds(4, 4)],
         yc_low.at[pl.ds(0, 4)], yc_high.at[pl.ds(0, 4)],
         yc_low.at[pl.ds(8, 4)], yc_high.at[pl.ds(8, 4)]],
    )
    blocks += [send_block(k) for k in (2, 6, 1, 7)]
    moved = []
    for i, step in enumerate((1, -1)):
        copy = pltpu.make_async_remote_copy(
            src_ref=movers.at[i],
            dst_ref=spec_out.at[pl.ds(n_depth * CAP + i * MIG, MIG), :],
            send_sem=mig_send.at[i],
            recv_sem=mig_recv.at[i],
            device_id=at(step, 0),
            device_id_type=MESH,
        )
        copy.start()
        moved.append(copy)
    for copy in third:
        copy.wait_recv()

    for p in range(4):
        cbuf[p, 0:16, :] = xc_low[p].astype(F32)
        cbuf[8 + p, 0:16, :] = xc_high[p].astype(F32)
    for p in range(12):
        cbuf[p, 16:24, :] = halo_rows(yc_high[p], yc_low[p])
    c_lane = iota((1, 256), 1)
    c_first = c_lane == 0
    c_last = c_lane == 255
    for p in range(12):
        dbuf[p] = (DAMPING / COARSE_CENTRE) * cbuf[p]

    def coarse_sweep(source_ref, target_ref, begin, end):
        def step(p, carry):
            value = source_ref[p]
            around = neighbour_sum(value, source_ref[p - 1], source_ref[p + 1], c_first, c_last)
            target_ref[p] = masked(
                value * (1.0 - DAMPING) + (DAMPING / COARSE_CENTRE) * (cbuf[p] + around)
            )
            return carry

        lax.fori_loop(begin, end, step, 0)

    coarse_sweep(dbuf, ebuf, 1, 11)
    coarse_sweep(ebuf, dbuf, 2, 10)
    coarse_sweep(dbuf, ebuf, 3, 9)

    fine_row = iota((40, 24), 0)
    from_row = jnp.where(fine_row < 36, lax.div(fine_row, 2), 22 + lax.div(fine_row - 36, 2))
    repeat_rows = jnp.where(from_row == iota((40, 24), 1), 1.0, 0.0)
    repeat_lanes = jnp.where(iota((256, 512), 0) == lax.div(iota((256, 512), 1), 2), 1.0, 0.0)
    spread = jnp.concatenate(
        [
            jnp.dot(repeat_rows, ebuf[3 + p], preferred_element_type=F32, precision=HIGHEST)
            for p in range(6)
        ],
        axis=0,
    )
    sbuf[...] = jnp.dot(
        spread, repeat_lanes, preferred_element_type=F32, precision=HIGHEST
    ).reshape(6, 40, 512)

    def correct(p, carry):
        addition = sbuf[p]
        ubuf[2 + 2 * p] = ubuf[2 + 2 * p] + addition
        ubuf[3 + 2 * p] = ubuf[3 + 2 * p] + addition
        return carry

    lax.fori_loop(0, 6, correct, 0)
    lax.fori_loop(3, 13, sweep_first, 0)

    def sweep_last(x, carry):
        value = vbuf[x]
        around = neighbour_sum(value, vbuf[x - 1], vbuf[x + 1], first_lane, last_lane)
        result = value * (1.0 - DAMPING) + (DAMPING / CENTRE) * (tbuf[x] + around)
        grid_out[x - 4] = result[0:32]
        return carry

    lax.fori_loop(4, 12, sweep_last, 0)

    for copy in blocks + moved:
        copy.wait_recv()
    for copy in first + second + third + blocks + moved:
        copy.wait_send()


def local(n_slab, n_depth, nutrient, species, agent_cell, death_flag, divide_flag, slab_move,
          depth_route, net_weight, sensing, uptake_weight):
    row = (1, ROWS)
    vmem = pl.BlockSpec(memory_space=pltpu.VMEM)
    scratch = [
        ((8, 32, 512), BF16), ((8, 4, 512), BF16), ((8, 4, 512), BF16),
        ((8, 32, 512), BF16), ((8, 4, 512), BF16), ((8, 4, 512), BF16),
        ((4, 16, 256), BF16), ((4, 4, 256), BF16), ((4, 4, 256), BF16),
        ((4, 32, 512), BF16), ((4, 32, 512), BF16), ((16, 4, 512), BF16), ((16, 4, 512), BF16),
        ((4, 32, 512), BF16), ((4, 32, 512), BF16), ((16, 4, 512), BF16), ((16, 4, 512), BF16),
        ((4, 16, 256), BF16), ((4, 16, 256), BF16), ((12, 4, 256), BF16), ((12, 4, 256), BF16),
        ((512, ROWS), BF16), ((ROWS, WIDTH), BF16), ((n_depth, CAP, WIDTH), BF16),
        ((2, MIG, WIDTH), BF16), ((6, 40, 512), F32),
        ((16, 40, 512), F32), ((16, 40, 512), F32), ((16, 40, 512), F32),
        ((8, 32, 512), F32), ((12, 24, 256), F32), ((12, 24, 256), F32), ((12, 24, 256), F32),
    ]
    return pl.pallas_call(
        functools.partial(kernel, n_slab, n_depth),
        out_shape=(
            jax.ShapeDtypeStruct((8, 32, 512), F32),
            jax.ShapeDtypeStruct((n_depth * CAP + 2 * MIG, WIDTH), BF16),
        ),
        in_specs=[vmem] * 10,
        out_specs=(vmem, vmem),
        scratch_shapes=[pltpu.VMEM(shape, dtype) for shape, dtype in scratch] + [
            pltpu.SemaphoreType.DMA((3, 8)), pltpu.SemaphoreType.DMA((3, 8)),
            pltpu.SemaphoreType.DMA((n_depth,)), pltpu.SemaphoreType.DMA((n_depth,)),
            pltpu.SemaphoreType.DMA((2,)), pltpu.SemaphoreType.DMA((2,)),
        ],
        compiler_params=pltpu.CompilerParams(
            collective_id=0, has_side_effects=True, vmem_limit_bytes=48 * 1024 * 1024
        ),
        name="step",
    )(
        nutrient, species, agent_cell.reshape(row), death_flag.reshape(row),
        divide_flag.reshape(row), slab_move.reshape(row), depth_route.reshape(row),
        net_weight, sensing.reshape(1, WIDTH), uptake_weight.reshape(1, WIDTH),
    )


def solution(mesh):
    in_specs = (
        P("slab", "depth", None),
        P(("slab", "depth"), None),
        P(("slab", "depth")),
        P(("slab", "depth")),
        P(("slab", "depth")),
        P(("slab", "depth")),
        P(("slab", "depth"), None),
        P(),
        P(),
        P(),
    )
    out_specs = (P("slab", "depth", None), P(("slab", "depth"), None))
    body = functools.partial(local, mesh.shape["slab"], mesh.shape["depth"])
    return jax.shard_map(body, mesh=mesh, in_specs=in_specs, out_specs=out_specs, check_vma=False)
```

time: 270 us -> 48.9 us (0.18)
  the two profiles are of different devices: /device:TPU:32 before, /device:TPU:1 now
where the time goes in v1:
time: 48.9 us; the launch traced here: 48.5 us
  Pallas kernels  41.4 us (85%)
  local copies, waits for them, and re-layouts  6.42 us (13%)
  between operations  0.69 us (1%)
    pallas_call x1, Pallas kernels, local(): pl.pallas_call(functools.partial(kernel, n_slab, n_depth), out_shape=(jax...  41.4 us
    unnamed x22, local copies, waits for them, and re-layouts  6.42 us

profile of v1, /device:TPU:1, one launch (start us, length us, event | category | flops | bytes accessed | tf_op | source)
XLA Modules:
  0.0 48.5 jit_solution(18059935959589191214)
XLA Ops:
  0.6 0.0 copy-start.5
  0.6 0.0 copy-start.4
  0.7 0.0 copy-start.3
  0.7 0.0 copy-start.8
  0.7 0.0 copy-start.9
  0.7 0.6 %copy-done.5 = s32[1024]{0:T(1024)S(1)} copy-done((s32[1024]{0:T(1024)S(1)}, s32[1024]{0:T(1024)}, u32[]{:S(2)}) %copy-start.5) | copy-done | bytes 4120
  1.3 0.0 copy-done.4
  1.3 0.0 copy-done.3
  1.4 0.0 copy-done.8
  1.4 0.0 copy-done.9
  1.4 0.0 copy-start
  1.4 1.0 %copy-done = f32[8,32,512]{2,1,0:T(8,128)S(1)} copy-done((f32[8,32,512]{2,1,0:T(8,128)S(1)}, f32[8,32,512]{2,1,0:T(8,128)}, u32[]{:S(2)}) %copy-start) | copy-done | bytes 524312
  2.4 0.0 copy-start.1
  2.4 0.9 %copy-done.1 = bf16[1024,128]{1,0:T(8,128)(2,1)S(1)} copy-done((bf16[1024,128]{1,0:T(8,128)(2,1)S(1)}, bf16[1024,128]{1,0:T(8,128)(2,1)}, u32[]{:S(2)}) %copy-start.1) | copy-done | bytes 262168
  3.4 0.0 copy-start.2
  3.4 0.8 %copy-done.2 = bf16[128,128]{1,0:T(8,128)(2,1)S(1)} copy-done((bf16[128,128]{1,0:T(8,128)(2,1)S(1)}, bf16[128,128]{1,0:T(8,128)(2,1)}, u32[]{:S(2)}) %copy-start.2) | copy-done | bytes 32792
  4.1 0.0 copy-start.6
  4.1 0.7 %copy-done.6 = s32[1024]{0:T(1024)S(1)} copy-done((s32[1024]{0:T(1024)S(1)}, s32[1024]{0:T(1024)}, u32[]{:S(2)}) %copy-start.6) | copy-done | bytes 4120
  4.8 0.0 copy-start.7
  4.8 0.7 %copy-done.7 = s32[1024,1]{0,1:T(1,128)S(1)} copy-done((s32[1024,1]{0,1:T(1,128)S(1)}, s32[1024,1]{0,1:T(1,128)}, u32[]{:S(2)}) %copy-start.7) | copy-done | bytes 4120
  5.5 41.4 %step.1 = (f32[8,32,512]{2,1,0:T(8,128)S(1)}, bf16[2304,128]{1,0:T(8,128)(2,1)S(1)}) custom-call(f32[8,32,512]{2,1,0:T(8,128)S(1)} %copy-done, bf16[1024,128]{1,0:T(8,128)(2,1)S(1)} %copy-done.1, s32[1,1024]{1,0:T(1,128)S(1)} %bitcast.7, s32[1,1024]{1,0:T(1,128)S(1)} %bitcast.8, s32[1,1024]{1,0:T(1,128)S(1)} %bitcast.9, s32[1,1024]{1,0:T(1,128)S(1)} %bitcast.10, ...), custom_call_target="tpu_custom_call" | custom-call | tf_op jit(solution)/shard_map/step/pallas_call | solution.py:379
  46.9 0.8 %copy.14 = f32[8,32,512]{2,1,0:T(8,128)} copy(f32[8,32,512]{2,1,0:T(8,128)S(1)} %get-tuple-element.4) | data formatting | bytes 1048576
  47.7 0.8 %copy.15 = bf16[2304,128]{1,0:T(8,128)(2,1)} copy(bf16[2304,128]{1,0:T(8,128)(2,1)S(1)} %get-tuple-element.5) | data formatting | bytes 1179648
Async XLA Ops:
  0.6 0.7 %copy-start.5 = (s32[1024]{0:T(1024)S(1)}, s32[1024]{0:T(1024)}, u32[]{:S(2)}) copy-start(s32[1024]{0:T(1024)} %param.14) | copy-start | bytes 12292
  0.6 0.7 %copy-start.4 = (s32[1024]{0:T(1024)S(1)}, s32[1024]{0:T(1024)}, u32[]{:S(2)}) copy-start(s32[1024]{0:T(1024)} %param.13) | copy-start | bytes 12292
  0.7 0.7 %copy-start.3 = (s32[1024]{0:T(1024)S(1)}, s32[1024]{0:T(1024)}, u32[]{:S(2)}) copy-start(s32[1024]{0:T(1024)} %param.12) | copy-start | bytes 12292
  0.7 0.7 %copy-start.8 = (f32[128]{0:T(128)S(1)}, f32[128]{0:T(128)}, u32[]{:S(2)}) copy-start(f32[128]{0:T(128)} %param.18) | copy-start | bytes 1540
  0.7 0.7 %copy-start.9 = (bf16[128]{0:T(256)(128)(2,1)S(1)}, bf16[128]{0:T(256)(128)(2,1)}, u32[]{:S(2)}) copy-start(bf16[128]{0:T(256)(128)(2,1)} %param.19) | copy-start | bytes 772
  1.4 1.0 %copy-start = (f32[8,32,512]{2,1,0:T(8,128)S(1)}, f32[8,32,512]{2,1,0:T(8,128)}, u32[]{:S(2)}) copy-start(f32[8,32,512]{2,1,0:T(8,128)} %nut.1) | copy-start | bytes 1572868
  2.4 0.9 %copy-start.1 = (bf16[1024,128]{1,0:T(8,128)(2,1)S(1)}, bf16[1024,128]{1,0:T(8,128)(2,1)}, u32[]{:S(2)}) copy-start(bf16[1024,128]{1,0:T(8,128)(2,1)} %spec.1) | copy-start | bytes 786436
  3.4 0.8 %copy-start.2 = (bf16[128,128]{1,0:T(8,128)(2,1)S(1)}, bf16[128,128]{1,0:T(8,128)(2,1)}, u32[]{:S(2)}) copy-start(bf16[128,128]{1,0:T(8,128)(2,1)} %netw.1) | copy-start | bytes 98308
  4.1 0.7 %copy-start.6 = (s32[1024]{0:T(1024)S(1)}, s32[1024]{0:T(1024)}, u32[]{:S(2)}) copy-start(s32[1024]{0:T(1024)} %param.15) | copy-start | bytes 12292
  4.8 0.7 %copy-start.7 = (s32[1024,1]{0,1:T(1,128)S(1)}, s32[1024,1]{0,1:T(1,128)}, u32[]{:S(2)}) copy-start(s32[1024,1]{0,1:T(1,128)} %param.16) | copy-start | bytes 12292

commit v2 on v1

v2 whole, which is shorter than its diff:
```python
import functools

import jax
import jax.numpy as jnp
from jax import lax
from jax.experimental import pallas as pl
from jax.experimental.pallas import tpu as pltpu
from jax.sharding import PartitionSpec as P

SCREENING = 0.05
DAMPING = 2.0 / 3.0
CENTRE = 6.0 + SCREENING
COARSE_CENTRE = 6.0 + 4.0 * SCREENING
F32 = jnp.float32
BF16 = jnp.bfloat16
I32 = jnp.int32
MESH = pl.DeviceIdType.MESH

ROWS = 1024
CAP = 256
MIG = 128
WIDTH = 128
SIDES = ((1, 0), (-1, 0), (0, 1), (0, -1), (1, 1), (1, -1), (-1, 1), (-1, -1))


def iota(shape, axis, dtype=I32):
    values = lax.broadcasted_iota(I32, shape, axis)
    return values if dtype == I32 else values.astype(dtype)


def tile_sweep(ref, x, tiles, first_row, rows, first_lane, last_lane):
    centre = [ref[x, z, pl.ds(first_row, rows), :] for z in range(tiles)]
    ahead = [pltpu.roll(value, 1, 1) for value in centre]
    back = [pltpu.roll(value, 127, 1) for value in centre]
    out = []
    for z in range(tiles):
        left = jnp.where(first_lane, ahead[z - 1] if z > 0 else 0.0, ahead[z])
        right = jnp.where(last_lane, back[z + 1] if z < tiles - 1 else 0.0, back[z])
        total = left + right
        total = total + ref[x, z, pl.ds(first_row - 1, rows), :]
        total = total + ref[x, z, pl.ds(first_row + 1, rows), :]
        total = total + ref[x - 1, z, pl.ds(first_row, rows), :]
        total = total + ref[x + 1, z, pl.ds(first_row, rows), :]
        out.append((centre[z], total))
    return out


def kernel(
    n_slab, n_depth,
    nut_in, spec_in, cell_in, death_in, divide_in, move_in, route_in, netw_in, sensing_in, uw_in,
    grid_out, spec_out,
    nut, spec, cell, death, divide, move, route, netw, sensing, uw,
    nb, nb_low, nb_high, src, src_low, src_high, cb, cb_low, cb_high,
    xr_low, xr_high, yr_low, yr_high,
    xs_low, xs_high, ys_low, ys_high,
    xc_low, xc_high, yc_low, yc_high,
    lane_hot, upd, packed, movers, sbuf, tbuf, ubuf, vbuf, wbuf, rbuf, cbuf, dbuf, ebuf,
    halo_send, halo_recv, a2a_send, a2a_recv, mig_send, mig_recv, in_sem,
):
    s = lax.axis_index("slab")
    d = lax.axis_index("depth")

    def at(step_s, step_d):
        return (lax.rem(s + step_s + n_slab, n_slab), lax.rem(d + step_d + n_depth, n_depth))

    barrier = pltpu.get_barrier_semaphore()
    partners = [at(a, b) for a, b in SIDES if a != 0] + [at(0, k) for k in range(1, n_depth)]
    for partner in partners:
        pl.semaphore_signal(barrier, inc=1, device_id=partner, device_id_type=MESH)

    loads = []
    for i, (source_ref, target_ref) in enumerate((
        (cell_in, cell), (nut_in, nut), (spec_in, spec), (uw_in, uw), (death_in, death),
        (divide_in, divide), (move_in, move), (route_in, route), (netw_in, netw),
        (sensing_in, sensing),
    )):
        load = pltpu.make_async_copy(source_ref, target_ref, in_sem.at[i])
        load.start()
        loads.append(load)

    def exchange(number, sources, targets):
        copies = []
        for i, (a, b) in enumerate(SIDES):
            copy = pltpu.make_async_remote_copy(
                src_ref=sources[i],
                dst_ref=targets[i],
                send_sem=halo_send.at[number, i],
                recv_sem=halo_recv.at[number, i],
                device_id=at(a, b),
                device_id_type=MESH,
            )
            copy.start()
            copies.append(copy)
        return copies

    loads[0].wait()
    cell_row = cell[...]
    z_row = lax.rem(cell_row, 512)
    xy_row = lax.div(cell_row, 512)

    def fill_lane(i, carry):
        start = pl.multiple_of(i * 64, 64)
        hit = iota((64, ROWS), 0) == z_row - start
        lane_hot[pl.ds(start, 64), :] = jnp.where(hit, 1.0, 0.0).astype(BF16)
        return carry

    lax.fori_loop(0, 8, fill_lane, 0)

    loads[1].wait()
    for x in range(8):
        plane = nut[x].astype(BF16)
        nb[x] = plane
        nb_low[x] = plane[0:4]
        nb_high[x] = plane[28:32]
    pl.semaphore_wait(barrier, len(partners))
    first = exchange(
        0,
        [nb.at[pl.ds(4, 4)], nb.at[pl.ds(0, 4)], nb_high, nb_low,
         nb_high.at[pl.ds(4, 4)], nb_low.at[pl.ds(4, 4)],
         nb_high.at[pl.ds(0, 4)], nb_low.at[pl.ds(0, 4)]],
        [xr_low, xr_high, yr_low.at[pl.ds(4, 8)], yr_high.at[pl.ds(4, 8)],
         yr_low.at[pl.ds(0, 4)], yr_high.at[pl.ds(0, 4)],
         yr_low.at[pl.ds(12, 4)], yr_high.at[pl.ds(12, 4)]],
    )

    sampled = jnp.dot(nb[...].reshape(256, 512), lane_hot[...], preferred_element_type=F32)
    row_hit = iota((256, ROWS), 0) == xy_row
    sample = jnp.sum(jnp.where(row_hit, sampled, 0.0), axis=0, keepdims=True)
    for load in loads[2:]:
        load.wait()
    alive = 1.0 - death[...].astype(F32)
    score = lax.dot_general(
        jnp.broadcast_to(uw[...], (16, WIDTH)), spec[...], (((1,), (1,)), ((), ())),
        preferred_element_type=F32,
    )[0:1]
    softplus = jnp.maximum(score, 0.0) + jnp.log1p(jnp.exp(-jnp.abs(score)))
    uptake = alive * (1.0 + divide[...].astype(F32)) * softplus * sample / (0.5 + sample)

    row_hit = iota((256, ROWS), 0) == xy_row
    source = lax.dot_general(
        jnp.where(row_hit, uptake, 0.0).astype(BF16), lane_hot[...], (((1,), (1,)), ((), ())),
        preferred_element_type=F32,
    ).reshape(8, 32, 512)
    for x in range(8):
        plane = source[x]
        rounded = plane.astype(BF16)
        src[x] = rounded
        src_low[x] = rounded[0:4]
        src_high[x] = rounded[28:32]
        target = SCREENING * nut[x] - plane
        for z in range(4):
            tbuf[4 + x, z, 12:44, :] = target[:, z * 128:(z + 1) * 128]
    second = exchange(
        1,
        [src.at[pl.ds(5, 3)], src.at[pl.ds(0, 3)], src_high, src_low,
         src_high.at[pl.ds(5, 3)], src_low.at[pl.ds(5, 3)],
         src_high.at[pl.ds(0, 3)], src_low.at[pl.ds(0, 3)]],
        [xs_low.at[pl.ds(1, 3)], xs_high.at[pl.ds(0, 3)],
         ys_low.at[pl.ds(4, 8)], ys_high.at[pl.ds(4, 8)],
         ys_low.at[pl.ds(1, 3)], ys_high.at[pl.ds(1, 3)],
         ys_low.at[pl.ds(12, 3)], ys_high.at[pl.ds(12, 3)]],
    )
    for x in range(8):
        for z in range(4):
            ubuf[4 + x, z, 12:44, :] = nut[x, :, z * 128:(z + 1) * 128]

    sensed = sample.astype(BF16).astype(F32)
    activation = jnp.dot(spec[...], netw[...], preferred_element_type=F32)
    sensed_column = jnp.transpose(jnp.broadcast_to(sensed, (WIDTH, ROWS)))
    activation = activation + sensed_column * sensing[...]
    upd[...] = (0.5 * spec[...].astype(F32) + jnp.tanh(activation)).astype(BF16)

    lanes = iota((16, ROWS), 0)
    move_row = move[...]
    route_row = route[...]
    counted = (lanes == route_row) | (lanes == 7 + move_row) & (move_row > 0)
    counted = jnp.where(counted, 1.0, 0.0)
    chosen = jnp.where(move_row == 0, route_row, 7 + move_row)
    stacked = jnp.concatenate([counted[:, a * 128:(a + 1) * 128] for a in range(8)], axis=0)
    before = jnp.where(iota((128, 128), 0) < iota((128, 128), 1), 1.0, 0.0)
    inside = jnp.dot(stacked.astype(BF16), before.astype(BF16), preferred_element_type=F32)
    total = jnp.dot(stacked.astype(BF16), jnp.ones((128, 128), BF16), preferred_element_type=F32)
    offset = jnp.zeros((16, 128), F32)
    ranks = []
    for a in range(8):
        ranks.append(inside[a * 16:(a + 1) * 16] + offset)
        offset = offset + total[a * 16:(a + 1) * 16]
    rank = jnp.concatenate(ranks, axis=1)
    rank = jnp.sum(jnp.where(lanes == chosen, rank, 0.0), axis=0, keepdims=True)
    rank = jnp.where(alive > 0.0, rank, -1.0)
    chosen = chosen.astype(F32)

    def pack(destination, slots):
        key = jnp.where(chosen == destination, rank, -1.0)
        hot = jnp.where(iota((slots, ROWS), 0, F32) == key, 1.0, 0.0).astype(BF16)
        return jnp.dot(hot, upd[...], preferred_element_type=F32).astype(BF16)

    def pack_step(k, carry):
        packed[k] = pack(lax.rem(d + k, n_depth).astype(F32), CAP)
        return carry

    lax.fori_loop(1, n_depth, pack_step, 0)
    movers[0] = pack(8.0, MIG)
    movers[1] = pack(9.0, MIG)
    own = pl.multiple_of(d * CAP, CAP)
    spec_out[pl.ds(own, CAP), :] = pack(d.astype(F32), CAP)

    def send_block(k):
        copy = pltpu.make_async_remote_copy(
            src_ref=packed.at[k],
            dst_ref=spec_out.at[pl.ds(own, CAP), :],
            send_sem=a2a_send.at[k],
            recv_sem=a2a_recv.at[k],
            device_id=at(0, k),
            device_id_type=MESH,
        )
        copy.start()
        return copy

    blocks = [send_block(k) for k in (4, 3, 5)]

    lane = iota((1, 128), 1)
    first_lane = lane == 0
    last_lane = lane == 127
    row8 = iota((8, 1), 0)
    keep_low = (row8 >= 4) | (d > 0)
    keep_high = (row8 < 4) | (d < n_depth - 1)
    has_low = jnp.full((4, 1), d, I32) > 0
    has_high = jnp.full((4, 1), d, I32) < n_depth - 1

    def fill_rows(x, with_source):
        low = jnp.where(has_low, yr_low[x].astype(F32), 0.0)
        high = jnp.where(has_high, yr_high[x].astype(F32), 0.0)
        for z in range(4):
            at_z = slice(z * 128, (z + 1) * 128)
            ubuf[x, z, 8:12, :] = low[:, at_z]
            ubuf[x, z, 44:48, :] = high[:, at_z]
        if with_source:
            low = SCREENING * low - ys_low[x].astype(F32)
            high = SCREENING * high - ys_high[x].astype(F32)
            for z in range(4):
                at_z = slice(z * 128, (z + 1) * 128)
                tbuf[x, z, 8:12, :] = low[:, at_z]
                tbuf[x, z, 44:48, :] = high[:, at_z]

    def masked(value, rows):
        return jnp.concatenate(
            [jnp.where(keep_low, value[0:8], 0.0), value[8:rows - 8],
             jnp.where(keep_high, value[rows - 8:], 0.0)], axis=0,
        )

    def sweep(source_ref, target_ref, x):
        for z, (value, around) in enumerate(
            tile_sweep(source_ref, x, 4, 8, 40, first_lane, last_lane)
        ):
            result = value * (1.0 - DAMPING) + (DAMPING / CENTRE) * (tbuf[x, z, 8:48, :] + around)
            target_ref[x, z, 8:48, :] = masked(result, 40)

    def residual(x):
        for z, (value, around) in enumerate(
            tile_sweep(wbuf, x, 4, 12, 32, first_lane, last_lane)
        ):
            rbuf[x - 4, z] = tbuf[x, z, 12:44, :] + around - CENTRE * value

    def loop(begin, end, step):
        lax.fori_loop(begin, end, lambda x, carry: (step(x), carry)[1], 0)

    for copy in (first[2], first[3], second[2], second[3]):
        copy.wait_recv()
    loop(4, 12, lambda x: fill_rows(x, True))
    loop(5, 11, lambda x: sweep(ubuf, vbuf, x))
    loop(6, 10, lambda x: sweep(vbuf, wbuf, x))
    loop(7, 9, residual)

    for i in (0, 1, 4, 5, 6, 7):
        first[i].wait_recv()
        second[i].wait_recv()

    def fill_plane(x, value, taken):
        value = value.astype(F32)
        for z in range(4):
            ubuf[x, z, 12:44, :] = value[:, z * 128:(z + 1) * 128]
        if taken is not None:
            value = SCREENING * value - taken.astype(F32)
            for z in range(4):
                tbuf[x, z, 12:44, :] = value[:, z * 128:(z + 1) * 128]
        fill_rows(x, taken is not None)

    fill_plane(0, xr_low[0], None)
    fill_plane(15, xr_high[3], None)

    def fill_outer(i):
        fill_plane(i, xr_low[i], xs_low[i])
        fill_plane(11 + i, xr_high[i - 1], xs_high[i - 1])

    loop(1, 4, fill_outer)

    def both(step, offset):
        def run(x):
            step(x)
            step(x + offset)
        return run

    loop(1, 5, both(lambda x: sweep(ubuf, vbuf, x), 10))
    loop(2, 6, both(lambda x: sweep(vbuf, wbuf, x), 8))
    loop(4, 7, both(residual, 5))

    def two_pieces(value, matrix):
        piece = value.astype(BF16)
        rest = (value - piece.astype(F32)).astype(BF16)
        product = jnp.dot(
            jnp.concatenate([piece, rest], axis=0), matrix, preferred_element_type=F32
        )
        return product[0:value.shape[0]] + product[value.shape[0]:]

    def pair_sum(p, z):
        total = None
        for x in (2 * p, 2 * p + 1):
            for r in (0, 1):
                part = rbuf[x, z, pl.ds(r, 16, stride=2), :]
                total = part if total is None else total + part
        return total

    lane_pairs = jnp.where(lax.div(iota((256, 128), 0), 2) == iota((256, 128), 1), 0.5, 0.0)
    lane_pairs = lane_pairs.astype(BF16)
    for h in range(2):
        sums = jnp.concatenate(
            [
                jnp.concatenate([pair_sum(p, 2 * h), pair_sum(p, 2 * h + 1)], axis=1)
                for p in range(4)
            ],
            axis=0,
        )
        coarse_target = two_pieces(sums, lane_pairs)
        at_h = slice(h * 128, (h + 1) * 128)
        for p in range(4):
            plane = coarse_target[p * 16:(p + 1) * 16]
            rounded = plane.astype(BF16)
            cb[p, :, at_h] = rounded
            cb_low[p, :, at_h] = rounded[0:4]
            cb_high[p, :, at_h] = rounded[12:16]
            cbuf[4 + p, h, 12:28, :] = plane
    third = exchange(
        2,
        [cb, cb, cb_high, cb_low, cb_high, cb_low, cb_high, cb_low],
        [xc_low, xc_high, yc_low.at[pl.ds(4, 4)], yc_high.at[pl.ds(4, 4)],
         yc_low.at[pl.ds(0, 4)], yc_high.at[pl.ds(0, 4)],
         yc_low.at[pl.ds(8, 4)], yc_high.at[pl.ds(8, 4)]],
    )
    blocks += [send_block(k) for k in (2, 6, 1, 7)]
    moved = []
    for i, step in enumerate((1, -1)):
        copy = pltpu.make_async_remote_copy(
            src_ref=movers.at[i],
            dst_ref=spec_out.at[pl.ds(n_depth * CAP + i * MIG, MIG), :],
            send_sem=mig_send.at[i],
            recv_sem=mig_recv.at[i],
            device_id=at(step, 0),
            device_id_type=MESH,
        )
        copy.start()
        moved.append(copy)
    for copy in third:
        copy.wait_recv()

    for p in range(12):
        low = jnp.where(has_low, yc_low[p].astype(F32), 0.0)
        high = jnp.where(has_high, yc_high[p].astype(F32), 0.0)
        for h in range(2):
            at_h = slice(h * 128, (h + 1) * 128)
            if p < 4:
                cbuf[p, h, 12:28, :] = xc_low[p, :, at_h].astype(F32)
            if p >= 8:
                cbuf[p, h, 12:28, :] = xc_high[p - 8, :, at_h].astype(F32)
            cbuf[p, h, 8:12, :] = low[:, at_h]
            cbuf[p, h, 28:32, :] = high[:, at_h]
    for p in range(12):
        for h in range(2):
            dbuf[p, h, 8:32, :] = (DAMPING / COARSE_CENTRE) * cbuf[p, h, 8:32, :]

    def coarse_sweep(source_ref, target_ref, p):
        for h, (value, around) in enumerate(
            tile_sweep(source_ref, p, 2, 8, 24, first_lane, last_lane)
        ):
            result = value * (1.0 - DAMPING) + (DAMPING / COARSE_CENTRE) * (
                cbuf[p, h, 8:32, :] + around
            )
            target_ref[p, h, 8:32, :] = masked(result, 24)

    loop(1, 6, both(lambda p: coarse_sweep(dbuf, ebuf, p), 5))
    loop(2, 6, both(lambda p: coarse_sweep(ebuf, dbuf, p), 4))
    loop(3, 6, both(lambda p: coarse_sweep(dbuf, ebuf, p), 3))

    repeat_lanes = jnp.where(iota((128, 256), 0) == lax.div(iota((128, 256), 1), 2), 1.0, 0.0)
    repeat_lanes = repeat_lanes.astype(BF16)
    for h in range(2):
        spread = two_pieces(
            jnp.concatenate([ebuf[3 + p, h, 10:34, :] for p in range(6)], axis=0), repeat_lanes
        )
        for p in range(6):
            for z in range(2):
                part = spread[p * 24:(p + 1) * 24, z * 128:(z + 1) * 128]
                sbuf[p, 2 * h + z, pl.ds(0, 24, stride=2), :] = part
                sbuf[p, 2 * h + z, pl.ds(1, 24, stride=2), :] = part

    def correct(p):
        for z in range(4):
            addition = sbuf[p, z, 0:40, :]
            for x in (2 + 2 * p, 3 + 2 * p):
                ubuf[x, z, 8:48, :] = wbuf[x, z, 8:48, :] + addition

    loop(0, 6, correct)
    loop(3, 8, both(lambda x: sweep(ubuf, vbuf, x), 5))

    def last_sweep(x):
        for z, (value, around) in enumerate(
            tile_sweep(vbuf, x, 4, 12, 32, first_lane, last_lane)
        ):
            grid_out[x - 4, :, z * 128:(z + 1) * 128] = value * (1.0 - DAMPING) + (
                DAMPING / CENTRE
            ) * (tbuf[x, z, 12:44, :] + around)

    loop(4, 8, both(last_sweep, 4))

    for copy in blocks + moved:
        copy.wait_recv()
    for copy in first + second + third + blocks + moved:
        copy.wait_send()


def local(n_slab, n_depth, nutrient, species, agent_cell, death_flag, divide_flag, slab_move,
          depth_route, net_weight, sensing, uptake_weight):
    row = (1, ROWS)
    vmem = pl.BlockSpec(memory_space=pltpu.VMEM)
    scratch = [
        ((8, 32, 512), F32), ((ROWS, WIDTH), BF16), (row, I32), (row, I32), (row, I32), (row, I32),
        (row, I32), ((WIDTH, WIDTH), BF16), ((1, WIDTH), F32), ((1, WIDTH), BF16),
        ((8, 32, 512), BF16), ((8, 4, 512), BF16), ((8, 4, 512), BF16),
        ((8, 32, 512), BF16), ((8, 4, 512), BF16), ((8, 4, 512), BF16),
        ((4, 16, 256), BF16), ((4, 4, 256), BF16), ((4, 4, 256), BF16),
        ((4, 32, 512), BF16), ((4, 32, 512), BF16), ((16, 4, 512), BF16), ((16, 4, 512), BF16),
        ((4, 32, 512), BF16), ((4, 32, 512), BF16), ((16, 4, 512), BF16), ((16, 4, 512), BF16),
        ((4, 16, 256), BF16), ((4, 16, 256), BF16), ((12, 4, 256), BF16), ((12, 4, 256), BF16),
        ((512, ROWS), BF16), ((ROWS, WIDTH), BF16), ((n_depth, CAP, WIDTH), BF16),
        ((2, MIG, WIDTH), BF16), ((6, 4, 48, 128), F32),
        ((16, 4, 56, 128), F32), ((16, 4, 56, 128), F32), ((16, 4, 56, 128), F32),
        ((16, 4, 56, 128), F32), ((8, 4, 32, 128), F32),
        ((12, 2, 40, 128), F32), ((12, 2, 40, 128), F32), ((12, 2, 40, 128), F32),
    ]
    return pl.pallas_call(
        functools.partial(kernel, n_slab, n_depth),
        out_shape=(
            jax.ShapeDtypeStruct((8, 32, 512), F32),
            jax.ShapeDtypeStruct((n_depth * CAP + 2 * MIG, WIDTH), BF16),
        ),
        in_specs=[pl.BlockSpec(memory_space=pltpu.HBM)] * 10,
        out_specs=(vmem, vmem),
        scratch_shapes=[pltpu.VMEM(shape, dtype) for shape, dtype in scratch] + [
            pltpu.SemaphoreType.DMA((3, 8)), pltpu.SemaphoreType.DMA((3, 8)),
            pltpu.SemaphoreType.DMA((n_depth,)), pltpu.SemaphoreType.DMA((n_depth,)),
            pltpu.SemaphoreType.DMA((2,)), pltpu.SemaphoreType.DMA((2,)),
            pltpu.SemaphoreType.DMA((10,)),
        ],
        compiler_params=pltpu.CompilerParams(
            collective_id=0, has_side_effects=True, vmem_limit_bytes=48 * 1024 * 1024
        ),
        name="step",
    )(
        *[pltpu.with_memory_space_constraint(v, pltpu.HBM) for v in (nutrient, species, agent_cell.reshape(row), death_flag.reshape(row),
        divide_flag.reshape(row), slab_move.reshape(row), depth_route.reshape(row),
        net_weight, sensing.reshape(1, WIDTH), uptake_weight.reshape(1, WIDTH))],
    )


def solution(mesh):
    in_specs = (
        P("slab", "depth", None),
        P(("slab", "depth"), None),
        P(("slab", "depth")),
        P(("slab", "depth")),
        P(("slab", "depth")),
        P(("slab", "depth")),
        P(("slab", "depth"), None),
        P(),
        P(),
        P(),
    )
    out_specs = (P("slab", "depth", None), P(("slab", "depth"), None))
    body = functools.partial(local, mesh.shape["slab"], mesh.shape["depth"])
    return jax.shard_map(body, mesh=mesh, in_specs=in_specs, out_specs=out_specs, check_vma=False)
```

time: 48.9 us -> 39 us (0.80)
  local copies, waits for them, and re-layouts: 6.42 us -> 1.61 us
  Pallas kernels: 41.4 us -> 36.6 us
    pallas_call x1, Pallas kernels: 41.4 us -> 36.6 us  [local(): pl.pallas_call(functools.partial(kernel, n_slab, n_depth), out_shape=(jax...]
    unnamed x22 -> x2, local copies, waits for them, and re-layouts: 6.42 us -> 1.61 us
where the time goes in v2:
time: 39 us; the launch traced here: 38.8 us
  Pallas kernels  36.6 us (94%)
  local copies, waits for them, and re-layouts  1.61 us (4%)
  between operations  0.64 us (2%)
    pallas_call x1, Pallas kernels, local(): pl.pallas_call(functools.partial(kernel, n_slab, n_depth), out_shape=(jax...  36.6 us
    unnamed x2, local copies, waits for them, and re-layouts  1.61 us

profile of v2, /device:TPU:1, one launch (start us, length us, event | category | flops | bytes accessed | tf_op | source)
XLA Modules:
  0.0 38.8 jit_solution(17622071889488544394)
XLA Ops:
  0.6 36.6 %step.1 = (f32[8,32,512]{2,1,0:T(8,128)S(1)}, bf16[2304,128]{1,0:T(8,128)(2,1)S(1)}) custom-call(f32[8,32,512]{2,1,0:T(8,128)} %nut_in.1, bf16[1024,128]{1,0:T(8,128)(2,1)} %spec_in.1, s32[1,1024]{1,0:T(1,128)} %bitcast.7, s32[1,1024]{1,0:T(1,128)} %bitcast.8, s32[1,1024]{1,0:T(1,128)} %bitcast.9, s32[1,1024]{1,0:T(1,128)} %bitcast.10, s32[1,1024]{1,0:T(1,128)} %bitcast.11, ...), custom_call_target="tpu_custom_call" | custom-call | tf_op jit(solution)/shard_map/step/pallas_call | solution.py:450
  37.2 0.8 %copy.14 = f32[8,32,512]{2,1,0:T(8,128)} copy(f32[8,32,512]{2,1,0:T(8,128)S(1)} %get-tuple-element.4) | data formatting | bytes 1048576
  38.0 0.8 %copy.15 = bf16[2304,128]{1,0:T(8,128)(2,1)} copy(bf16[2304,128]{1,0:T(8,128)(2,1)S(1)} %get-tuple-element.5) | data formatting | bytes 1179648

commit v3 on v2

--- a/solution.py
+++ b/solution.py
@@ -21,6 +21,7 @@
 MIG = 128
 WIDTH = 128
 SIDES = ((1, 0), (-1, 0), (0, 1), (0, -1), (1, 1), (1, -1), (-1, 1), (-1, -1))
+ORDER = (4, 5, 6, 7, 0, 1, 2, 3)
 
 
 def iota(shape, axis, dtype=I32):
@@ -30,13 +31,12 @@
 
 def tile_sweep(ref, x, tiles, first_row, rows, first_lane, last_lane):
     centre = [ref[x, z, pl.ds(first_row, rows), :] for z in range(tiles)]
-    ahead = [pltpu.roll(value, 1, 1) for value in centre]
-    back = [pltpu.roll(value, 127, 1) for value in centre]
+    before_first = jnp.where(first_lane, 0.0, pltpu.roll(centre[-1], 1, 1))
+    after_last = jnp.where(last_lane, 0.0, pltpu.roll(centre[0], 127, 1))
     out = []
     for z in range(tiles):
-        left = jnp.where(first_lane, ahead[z - 1] if z > 0 else 0.0, ahead[z])
-        right = jnp.where(last_lane, back[z + 1] if z < tiles - 1 else 0.0, back[z])
-        total = left + right
+        total = centre[z - 1] if z > 0 else before_first
+        total = total + (centre[z + 1] if z < tiles - 1 else after_last)
         total = total + ref[x, z, pl.ds(first_row - 1, rows), :]
         total = total + ref[x, z, pl.ds(first_row + 1, rows), :]
         total = total + ref[x - 1, z, pl.ds(first_row, rows), :]
@@ -48,13 +48,13 @@
 def kernel(
     n_slab, n_depth,
     nut_in, spec_in, cell_in, death_in, divide_in, move_in, route_in, netw_in, sensing_in, uw_in,
-    grid_out, spec_out,
-    nut, spec, cell, death, divide, move, route, netw, sensing, uw,
+    grid_out, spec_out, order,
+    own_nb, nut, spec, cell, death, divide, move, route, netw, sensing, uw,
     nb, nb_low, nb_high, src, src_low, src_high, cb, cb_low, cb_high,
     xr_low, xr_high, yr_low, yr_high,
     xs_low, xs_high, ys_low, ys_high,
     xc_low, xc_high, yc_low, yc_high,
-    lane_hot, upd, packed, movers, sbuf, tbuf, ubuf, vbuf, wbuf, rbuf, cbuf, dbuf, ebuf,
+    lane_hot, cell_hot, upd, packed, movers, sbuf, tbuf, ubuf, vbuf, wbuf, rbuf, cbuf, dbuf, ebuf,
     halo_send, halo_recv, a2a_send, a2a_recv, mig_send, mig_recv, in_sem,
 ):
     s = lax.axis_index("slab")
@@ -79,8 +79,9 @@
         loads.append(load)
 
     def exchange(number, sources, targets):
-        copies = []
-        for i, (a, b) in enumerate(SIDES):
+        copies = {}
+        for i in ORDER:
+            a, b = SIDES[i]
             copy = pltpu.make_async_remote_copy(
                 src_ref=sources[i],
                 dst_ref=targets[i],
@@ -90,25 +91,34 @@
                 device_id_type=MESH,
             )
             copy.start()
-            copies.append(copy)
-        return copies
+            copies[i] = copy
+        return [copies[i] for i in range(len(SIDES))]
 
     loads[0].wait()
     cell_row = cell[...]
     z_row = lax.rem(cell_row, 512)
     xy_row = lax.div(cell_row, 512)
+    place_row = lax.rem(z_row, 4) * 128 + lax.div(z_row, 4)
+    places = iota((1, 512), 1)
+    cell_of_place = lax.rem(places, 128) * 4 + lax.div(places, 128)
 
     def fill_lane(i, carry):
         start = pl.multiple_of(i * 64, 64)
         hit = iota((64, ROWS), 0) == z_row - start
         lane_hot[pl.ds(start, 64), :] = jnp.where(hit, 1.0, 0.0).astype(BF16)
+        hit = iota((64, ROWS), 0) == place_row - start
+        cell_hot[pl.ds(start, 64), :] = jnp.where(hit, 1.0, 0.0).astype(BF16)
+        hit = iota((64, 512), 0) == cell_of_place - start
+        order[pl.ds(start, 64), :] = jnp.where(hit, 1.0, 0.0).astype(BF16)
         return carry
 
     lax.fori_loop(0, 8, fill_lane, 0)
 
     loads[1].wait()
+    own_nb[...] = nut[...].reshape(256, 512).astype(BF16)
+    placed = jnp.dot(own_nb[...], order[...], preferred_element_type=F32).astype(BF16)
     for x in range(8):
-        plane = nut[x].astype(BF16)
+        plane = placed[x * 32:(x + 1) * 32]
         nb[x] = plane
         nb_low[x] = plane[0:4]
         nb_high[x] = plane[28:32]
@@ -116,14 +126,14 @@
     first = exchange(
         0,
         [nb.at[pl.ds(4, 4)], nb.at[pl.ds(0, 4)], nb_high, nb_low,
-         nb_high.at[pl.ds(4, 4)], nb_low.at[pl.ds(4, 4)],
-         nb_high.at[pl.ds(0, 4)], nb_low.at[pl.ds(0, 4)]],
+         nb_high.at[pl.ds(5, 3)], nb_low.at[pl.ds(5, 3)],
+         nb_high.at[pl.ds(0, 3)], nb_low.at[pl.ds(0, 3)]],
         [xr_low, xr_high, yr_low.at[pl.ds(4, 8)], yr_high.at[pl.ds(4, 8)],
-         yr_low.at[pl.ds(0, 4)], yr_high.at[pl.ds(0, 4)],
-         yr_low.at[pl.ds(12, 4)], yr_high.at[pl.ds(12, 4)]],
+         yr_low.at[pl.ds(1, 3)], yr_high.at[pl.ds(1, 3)],
+         yr_low.at[pl.ds(12, 3)], yr_high.at[pl.ds(12, 3)]],
     )
 
-    sampled = jnp.dot(nb[...].reshape(256, 512), lane_hot[...], preferred_element_type=F32)
+    sampled = jnp.dot(own_nb[...], lane_hot[...], preferred_element_type=F32)
     row_hit = iota((256, ROWS), 0) == xy_row
     sample = jnp.sum(jnp.where(row_hit, sampled, 0.0), axis=0, keepdims=True)
     for load in loads[2:]:
@@ -138,7 +148,7 @@
 
     row_hit = iota((256, ROWS), 0) == xy_row
     source = lax.dot_general(
-        jnp.where(row_hit, uptake, 0.0).astype(BF16), lane_hot[...], (((1,), (1,)), ((), ())),
+        jnp.where(row_hit, uptake, 0.0).astype(BF16), cell_hot[...], (((1,), (1,)), ((), ())),
         preferred_element_type=F32,
     ).reshape(8, 32, 512)
     for x in range(8):
@@ -147,22 +157,32 @@
         src[x] = rounded
         src_low[x] = rounded[0:4]
         src_high[x] = rounded[28:32]
-        target = SCREENING * nut[x] - plane
         for z in range(4):
-            tbuf[4 + x, z, 12:44, :] = target[:, z * 128:(z + 1) * 128]
+            tbuf[4 + x, z, 12:44, :] = plane[:, z * 128:(z + 1) * 128]
     second = exchange(
         1,
         [src.at[pl.ds(5, 3)], src.at[pl.ds(0, 3)], src_high, src_low,
-         src_high.at[pl.ds(5, 3)], src_low.at[pl.ds(5, 3)],
-         src_high.at[pl.ds(0, 3)], src_low.at[pl.ds(0, 3)]],
+         src_high.at[pl.ds(6, 2)], src_low.at[pl.ds(6, 2)],
+         src_high.at[pl.ds(0, 2)], src_low.at[pl.ds(0, 2)]],
         [xs_low.at[pl.ds(1, 3)], xs_high.at[pl.ds(0, 3)],
          ys_low.at[pl.ds(4, 8)], ys_high.at[pl.ds(4, 8)],
-         ys_low.at[pl.ds(1, 3)], ys_high.at[pl.ds(1, 3)],
-         ys_low.at[pl.ds(12, 3)], ys_high.at[pl.ds(12, 3)]],
+         ys_low.at[pl.ds(2, 2)], ys_high.at[pl.ds(2, 2)],
+         ys_low.at[pl.ds(12, 2)], ys_high.at[pl.ds(12, 2)]],
     )
-    for x in range(8):
-        for z in range(4):
-            ubuf[4 + x, z, 12:44, :] = nut[x, :, z * 128:(z + 1) * 128]
+    for half in range(2):
+        value = nut[4 * half:4 * half + 4].reshape(128, 512)
+        rest = value - value.astype(BF16).astype(F32)
+        piece = rest.astype(BF16)
+        pieces = jnp.concatenate([piece, (rest - piece.astype(F32)).astype(BF16)], axis=0)
+        rest = jnp.dot(pieces, order[...], preferred_element_type=F32)
+        rest = rest[0:128] + rest[128:256]
+        for i in range(4):
+            x = 4 * half + i
+            value = nb[x].astype(F32) + rest[i * 32:(i + 1) * 32]
+            for z in range(4):
+                part = value[:, z * 128:(z + 1) * 128]
+                ubuf[4 + x, z, 12:44, :] = part
+                tbuf[4 + x, z, 12:44, :] = SCREENING * part - tbuf[4 + x, z, 12:44, :]
 
     sensed = sample.astype(BF16).astype(F32)
     activation = jnp.dot(spec[...], netw[...], preferred_element_type=F32)
@@ -305,14 +325,6 @@
     loop(2, 6, both(lambda x: sweep(vbuf, wbuf, x), 8))
     loop(4, 7, both(residual, 5))
 
-    def two_pieces(value, matrix):
-        piece = value.astype(BF16)
-        rest = (value - piece.astype(F32)).astype(BF16)
-        product = jnp.dot(
-            jnp.concatenate([piece, rest], axis=0), matrix, preferred_element_type=F32
-        )
-        return product[0:value.shape[0]] + product[value.shape[0]:]
-
     def pair_sum(p, z):
         total = None
         for x in (2 * p, 2 * p + 1):
@@ -321,20 +333,10 @@
                 total = part if total is None else total + part
         return total
 
-    lane_pairs = jnp.where(lax.div(iota((256, 128), 0), 2) == iota((256, 128), 1), 0.5, 0.0)
-    lane_pairs = lane_pairs.astype(BF16)
     for h in range(2):
-        sums = jnp.concatenate(
-            [
-                jnp.concatenate([pair_sum(p, 2 * h), pair_sum(p, 2 * h + 1)], axis=1)
-                for p in range(4)
-            ],
-            axis=0,
-        )
-        coarse_target = two_pieces(sums, lane_pairs)
         at_h = slice(h * 128, (h + 1) * 128)
         for p in range(4):
-            plane = coarse_target[p * 16:(p + 1) * 16]
+            plane = 0.5 * (pair_sum(p, 2 * h) + pair_sum(p, 2 * h + 1))
             rounded = plane.astype(BF16)
             cb[p, :, at_h] = rounded
             cb_low[p, :, at_h] = rounded[0:4]
@@ -391,23 +393,18 @@
     loop(2, 6, both(lambda p: coarse_sweep(ebuf, dbuf, p), 4))
     loop(3, 6, both(lambda p: coarse_sweep(dbuf, ebuf, p), 3))
 
-    repeat_lanes = jnp.where(iota((128, 256), 0) == lax.div(iota((128, 256), 1), 2), 1.0, 0.0)
-    repeat_lanes = repeat_lanes.astype(BF16)
-    for h in range(2):
-        spread = two_pieces(
-            jnp.concatenate([ebuf[3 + p, h, 10:34, :] for p in range(6)], axis=0), repeat_lanes
-        )
-        for p in range(6):
-            for z in range(2):
-                part = spread[p * 24:(p + 1) * 24, z * 128:(z + 1) * 128]
-                sbuf[p, 2 * h + z, pl.ds(0, 24, stride=2), :] = part
-                sbuf[p, 2 * h + z, pl.ds(1, 24, stride=2), :] = part
+    for p in range(6):
+        for h in range(2):
+            part = ebuf[3 + p, h, 10:34, :]
+            sbuf[p, h, pl.ds(0, 24, stride=2), :] = part
+            sbuf[p, h, pl.ds(1, 24, stride=2), :] = part
 
     def correct(p):
-        for z in range(4):
-            addition = sbuf[p, z, 0:40, :]
+        for h in range(2):
+            addition = sbuf[p, h, 0:40, :]
             for x in (2 + 2 * p, 3 + 2 * p):
-                ubuf[x, z, 8:48, :] = wbuf[x, z, 8:48, :] + addition
+                for z in (2 * h, 2 * h + 1):
+                    ubuf[x, z, 8:48, :] = wbuf[x, z, 8:48, :] + addition
 
     loop(0, 6, correct)
     loop(3, 8, both(lambda x: sweep(ubuf, vbuf, x), 5))
@@ -428,11 +425,31 @@
         copy.wait_send()
 
 
+def finish(placed, species_next, order, grid_out, spec_out, grid, sem):
+    copies = [pltpu.make_async_copy(species_next, spec_out, sem.at[0])]
+    copies[0].start()
+    for half in range(2):
+        value = placed[4 * half:4 * half + 4].reshape(128, 512)
+        piece = value.astype(BF16)
+        rest = (value - piece.astype(F32)).astype(BF16)
+        both = lax.dot_general(
+            jnp.concatenate([piece, rest], axis=0), order[...], (((1,), (1,)), ((), ())),
+            preferred_element_type=F32,
+        )
+        grid[4 * half:4 * half + 4] = (both[0:128] + both[128:256]).reshape(4, 32, 512)
+        at_half = pl.ds(4 * half, 4)
+        copies.append(pltpu.make_async_copy(grid.at[at_half], grid_out.at[at_half], sem.at[1 + half]))
+        copies[-1].start()
+    for copy in copies:
+        copy.wait()
+
+
 def local(n_slab, n_depth, nutrient, species, agent_cell, death_flag, divide_flag, slab_move,
           depth_route, net_weight, sensing, uptake_weight):
     row = (1, ROWS)
     vmem = pl.BlockSpec(memory_space=pltpu.VMEM)
     scratch = [
+        ((256, 512), BF16),
         ((8, 32, 512), F32), ((ROWS, WIDTH), BF16), (row, I32), (row, I32), (row, I32), (row, I32),
         (row, I32), ((WIDTH, WIDTH), BF16), ((1, WIDTH), F32), ((1, WIDTH), BF16),
         ((8, 32, 512), BF16), ((8, 4, 512), BF16), ((8, 4, 512), BF16),
@@ -441,20 +458,21 @@
         ((4, 32, 512), BF16), ((4, 32, 512), BF16), ((16, 4, 512), BF16), ((16, 4, 512), BF16),
         ((4, 32, 512), BF16), ((4, 32, 512), BF16), ((16, 4, 512), BF16), ((16, 4, 512), BF16),
         ((4, 16, 256), BF16), ((4, 16, 256), BF16), ((12, 4, 256), BF16), ((12, 4, 256), BF16),
-        ((512, ROWS), BF16), ((ROWS, WIDTH), BF16), ((n_depth, CAP, WIDTH), BF16),
-        ((2, MIG, WIDTH), BF16), ((6, 4, 48, 128), F32),
+        ((512, ROWS), BF16), ((512, ROWS), BF16), ((ROWS, WIDTH), BF16), ((n_depth, CAP, WIDTH), BF16),
+        ((2, MIG, WIDTH), BF16), ((6, 2, 48, 128), F32),
         ((16, 4, 56, 128), F32), ((16, 4, 56, 128), F32), ((16, 4, 56, 128), F32),
         ((16, 4, 56, 128), F32), ((8, 4, 32, 128), F32),
         ((12, 2, 40, 128), F32), ((12, 2, 40, 128), F32), ((12, 2, 40, 128), F32),
     ]
-    return pl.pallas_call(
+    placed, species_next, order = pl.pallas_call(
         functools.partial(kernel, n_slab, n_depth),
         out_shape=(
             jax.ShapeDtypeStruct((8, 32, 512), F32),
             jax.ShapeDtypeStruct((n_depth * CAP + 2 * MIG, WIDTH), BF16),
+            jax.ShapeDtypeStruct((512, 512), BF16),
         ),
         in_specs=[pl.BlockSpec(memory_space=pltpu.HBM)] * 10,
-        out_specs=(vmem, vmem),
+        out_specs=(vmem, vmem, vmem),
         scratch_shapes=[pltpu.VMEM(shape, dtype) for shape, dtype in scratch] + [
             pltpu.SemaphoreType.DMA((3, 8)), pltpu.SemaphoreType.DMA((3, 8)),
             pltpu.SemaphoreType.DMA((n_depth,)), pltpu.SemaphoreType.DMA((n_depth,)),
@@ -470,6 +488,18 @@
         divide_flag.reshape(row), slab_move.reshape(row), depth_route.reshape(row),
         net_weight, sensing.reshape(1, WIDTH), uptake_weight.reshape(1, WIDTH))],
     )
+    return pl.pallas_call(
+        finish,
+        out_shape=(
+            jax.ShapeDtypeStruct((8, 32, 512), F32),
+            jax.ShapeDtypeStruct((n_depth * CAP + 2 * MIG, WIDTH), BF16),
+        ),
+        in_specs=[vmem] * 3,
+        out_specs=(pl.BlockSpec(memory_space=pl.ANY), pl.BlockSpec(memory_space=pl.ANY)),
+        scratch_shapes=[pltpu.VMEM((8, 32, 512), F32), pltpu.SemaphoreType.DMA((3,))],
+        compiler_params=pltpu.CompilerParams(vmem_limit_bytes=16 * 1024 * 1024),
+        name="finish",
+    )(placed, species_next, order)
 
 
 def solution(mesh):

time: 39 us -> 36.2 us (0.928)
  local copies, waits for them, and re-layouts: 1.61 us -> 0 us
  Pallas kernels: 36.6 us -> 35.5 us
    pallas_call x1, Pallas kernels: 36.6 us -> 34.2 us  [local(): pl.pallas_call(functools.partial(kernel, n_slab, n_depth), out_shape=(jax...]
    unnamed x2 -> x0, local copies, waits for them, and re-layouts: 1.61 us -> none
    pallas_call x0 -> x1, Pallas kernels: none -> 1.2 us  [local(): pl.pallas_call(finish, out_shape=(jax.ShapeDtypeStruct((8, 32, 512), F32)...]
where the time goes in v3:
time: 36.2 us; the launch traced here: 36.1 us
  Pallas kernels  35.5 us (98%)
  between operations  0.64 us (2%)
    pallas_call x1, Pallas kernels, local(): pl.pallas_call(functools.partial(kernel, n_slab, n_depth), out_shape=(jax...  34.2 us
    pallas_call x1, Pallas kernels, local(): pl.pallas_call(finish, out_shape=(jax.ShapeDtypeStruct((8, 32, 512), F32)...  1.2 us

profile of v3, /device:TPU:1, one launch (start us, length us, event | category | flops | bytes accessed | tf_op | source)
XLA Modules:
  0.0 36.1 jit_solution(15863412509936901505)
XLA Ops:
  0.6 34.2 %step.1 = (f32[8,32,512]{2,1,0:T(8,128)S(1)}, bf16[2304,128]{1,0:T(8,128)(2,1)S(1)}, bf16[512,512]{1,0:T(8,128)(2,1)S(1)}) custom-call(f32[8,32,512]{2,1,0:T(8,128)} %nut_in.1, bf16[1024,128]{1,0:T(8,128)(2,1)} %spec_in.1, s32[1,1024]{1,0:T(1,128)} %bitcast.7, s32[1,1024]{1,0:T(1,128)} %bitcast.8, s32[1,1024]{1,0:T(1,128)} %bitcast.9, s32[1,1024]{1,0:T(1,128)} %bitcast.10, ...), custom_call_target="tpu_custom_call" | custom-call | tf_op jit(solution)/shard_map/step/pallas_call | solution.py:467
  34.9 1.2 %finish.1 = (f32[8,32,512]{2,1,0:T(8,128)}, bf16[2304,128]{1,0:T(8,128)(2,1)}) custom-call(f32[8,32,512]{2,1,0:T(8,128)S(1)} %get-tuple-element.5.placed, bf16[2304,128]{1,0:T(8,128)(2,1)S(1)} %get-tuple-element.6.species_next, bf16[512,512]{1,0:T(8,128)(2,1)S(1)} %get-tuple-element.7.order), custom_call_target="tpu_custom_call" | custom-call | tf_op jit(solution)/shard_map/finish/pallas_call | solution.py:491

commit v4 on v3

--- a/solution.py
+++ b/solution.py
@@ -55,7 +55,7 @@
     xs_low, xs_high, ys_low, ys_high,
     xc_low, xc_high, yc_low, yc_high,
     lane_hot, cell_hot, upd, packed, movers, sbuf, tbuf, ubuf, vbuf, wbuf, rbuf, cbuf, dbuf, ebuf,
-    halo_send, halo_recv, a2a_send, a2a_recv, mig_send, mig_recv, in_sem,
+    sampled_row, halo_send, halo_recv, a2a_send, a2a_recv, mig_send, mig_recv, in_sem,
 ):
     s = lax.axis_index("slab")
     d = lax.axis_index("depth")
@@ -122,6 +122,83 @@
         nb[x] = plane
         nb_low[x] = plane[0:4]
         nb_high[x] = plane[28:32]
+    for load in loads[2:]:
+        load.wait()
+    own = pl.multiple_of(d * CAP, CAP)
+
+    def gather_and_scatter():
+        sampled = jnp.dot(own_nb[...], lane_hot[...], preferred_element_type=F32)
+        row_hit = iota((256, ROWS), 0) == xy_row
+        sample = jnp.sum(jnp.where(row_hit, sampled, 0.0), axis=0, keepdims=True)
+        sampled_row[...] = sample
+        alive = 1.0 - death[...].astype(F32)
+        score = lax.dot_general(
+            jnp.broadcast_to(uw[...], (16, WIDTH)), spec[...], (((1,), (1,)), ((), ())),
+            preferred_element_type=F32,
+        )[0:1]
+        softplus = jnp.maximum(score, 0.0) + jnp.log1p(jnp.exp(-jnp.abs(score)))
+        uptake = alive * (1.0 + divide[...].astype(F32)) * softplus * sample / (0.5 + sample)
+
+        row_hit = iota((256, ROWS), 0) == xy_row
+        source = lax.dot_general(
+            jnp.where(row_hit, uptake, 0.0).astype(BF16), cell_hot[...], (((1,), (1,)), ((), ())),
+            preferred_element_type=F32,
+        ).reshape(8, 32, 512)
+        for x in range(8):
+            plane = source[x]
+            rounded = plane.astype(BF16)
+            src[x] = rounded
+            src_low[x] = rounded[0:4]
+            src_high[x] = rounded[28:32]
+            for z in range(4):
+                tbuf[4 + x, z, 12:44, :] = plane[:, z * 128:(z + 1) * 128]
+
+    def species_work():
+        sensed = sampled_row[...].astype(BF16).astype(F32)
+        activation = jnp.dot(spec[...], netw[...], preferred_element_type=F32)
+        sensed_column = jnp.transpose(jnp.broadcast_to(sensed, (WIDTH, ROWS)))
+        activation = activation + sensed_column * sensing[...]
+        upd[...] = (0.5 * spec[...].astype(F32) + jnp.tanh(activation)).astype(BF16)
+
+        lanes = iota((16, ROWS), 0)
+        move_row = move[...]
+        route_row = route[...]
+        counted = (lanes == route_row) | (lanes == 7 + move_row) & (move_row > 0)
+        counted = jnp.where(counted, 1.0, 0.0)
+        chosen = jnp.where(move_row == 0, route_row, 7 + move_row)
+        stacked = jnp.concatenate([counted[:, a * 128:(a + 1) * 128] for a in range(8)], axis=0)
+        before = jnp.where(iota((128, 128), 0) < iota((128, 128), 1), 1.0, 0.0)
+        inside = jnp.dot(stacked.astype(BF16), before.astype(BF16), preferred_element_type=F32)
+        total = jnp.dot(stacked.astype(BF16), jnp.ones((128, 128), BF16), preferred_element_type=F32)
+        offset = jnp.zeros((16, 128), F32)
+        ranks = []
+        for a in range(8):
+            ranks.append(inside[a * 16:(a + 1) * 16] + offset)
+            offset = offset + total[a * 16:(a + 1) * 16]
+        rank = jnp.concatenate(ranks, axis=1)
+        rank = jnp.sum(jnp.where(lanes == chosen, rank, 0.0), axis=0, keepdims=True)
+        rank = jnp.where(death[...] == 0, rank, -1.0)
+        chosen = chosen.astype(F32)
+
+        def pack(destination, slots):
+            key = jnp.where(chosen == destination, rank, -1.0)
+            hot = jnp.where(iota((slots, ROWS), 0, F32) == key, 1.0, 0.0).astype(BF16)
+            return jnp.dot(hot, upd[...], preferred_element_type=F32).astype(BF16)
+
+        def pack_step(k, carry):
+            packed[k] = pack(lax.rem(d + k, n_depth).astype(F32), CAP)
+            return carry
+
+        lax.fori_loop(1, n_depth, pack_step, 0)
+        movers[0] = pack(8.0, MIG)
+        movers[1] = pack(9.0, MIG)
+        spec_out[pl.ds(own, CAP), :] = pack(d.astype(F32), CAP)
+
+    early = s == 0
+    later = s > 0
+    pl.when(early)(gather_and_scatter)
+    pl.when(early & (d > 0))(species_work)
+
     pl.semaphore_wait(barrier, len(partners))
     first = exchange(
         0,
@@ -133,32 +210,7 @@
          yr_low.at[pl.ds(12, 3)], yr_high.at[pl.ds(12, 3)]],
     )
 
-    sampled = jnp.dot(own_nb[...], lane_hot[...], preferred_element_type=F32)
-    row_hit = iota((256, ROWS), 0) == xy_row
-    sample = jnp.sum(jnp.where(row_hit, sampled, 0.0), axis=0, keepdims=True)
-    for load in loads[2:]:
-        load.wait()
-    alive = 1.0 - death[...].astype(F32)
-    score = lax.dot_general(
-        jnp.broadcast_to(uw[...], (16, WIDTH)), spec[...], (((1,), (1,)), ((), ())),
-        preferred_element_type=F32,
-    )[0:1]
-    softplus = jnp.maximum(score, 0.0) + jnp.log1p(jnp.exp(-jnp.abs(score)))
-    uptake = alive * (1.0 + divide[...].astype(F32)) * softplus * sample / (0.5 + sample)
-
-    row_hit = iota((256, ROWS), 0) == xy_row
-    source = lax.dot_general(
-        jnp.where(row_hit, uptake, 0.0).astype(BF16), cell_hot[...], (((1,), (1,)), ((), ())),
-        preferred_element_type=F32,
-    ).reshape(8, 32, 512)
-    for x in range(8):
-        plane = source[x]
-        rounded = plane.astype(BF16)
-        src[x] = rounded
-        src_low[x] = rounded[0:4]
-        src_high[x] = rounded[28:32]
-        for z in range(4):
-            tbuf[4 + x, z, 12:44, :] = plane[:, z * 128:(z + 1) * 128]
+    pl.when(later)(gather_and_scatter)
     second = exchange(
         1,
         [src.at[pl.ds(5, 3)], src.at[pl.ds(0, 3)], src_high, src_low,
@@ -184,49 +236,10 @@
                 ubuf[4 + x, z, 12:44, :] = part
                 tbuf[4 + x, z, 12:44, :] = SCREENING * part - tbuf[4 + x, z, 12:44, :]
 
-    sensed = sample.astype(BF16).astype(F32)
-    activation = jnp.dot(spec[...], netw[...], preferred_element_type=F32)
-    sensed_column = jnp.transpose(jnp.broadcast_to(sensed, (WIDTH, ROWS)))
-    activation = activation + sensed_column * sensing[...]
-    upd[...] = (0.5 * spec[...].astype(F32) + jnp.tanh(activation)).astype(BF16)
-
-    lanes = iota((16, ROWS), 0)
-    move_row = move[...]
-    route_row = route[...]
-    counted = (lanes == route_row) | (lanes == 7 + move_row) & (move_row > 0)
-    counted = jnp.where(counted, 1.0, 0.0)
-    chosen = jnp.where(move_row == 0, route_row, 7 + move_row)
-    stacked = jnp.concatenate([counted[:, a * 128:(a + 1) * 128] for a in range(8)], axis=0)
-    before = jnp.where(iota((128, 128), 0) < iota((128, 128), 1), 1.0, 0.0)
-    inside = jnp.dot(stacked.astype(BF16), before.astype(BF16), preferred_element_type=F32)
-    total = jnp.dot(stacked.astype(BF16), jnp.ones((128, 128), BF16), preferred_element_type=F32)
-    offset = jnp.zeros((16, 128), F32)
-    ranks = []
-    for a in range(8):
-        ranks.append(inside[a * 16:(a + 1) * 16] + offset)
-        offset = offset + total[a * 16:(a + 1) * 16]
-    rank = jnp.concatenate(ranks, axis=1)
-    rank = jnp.sum(jnp.where(lanes == chosen, rank, 0.0), axis=0, keepdims=True)
-    rank = jnp.where(alive > 0.0, rank, -1.0)
-    chosen = chosen.astype(F32)
-
-    def pack(destination, slots):
-        key = jnp.where(chosen == destination, rank, -1.0)
-        hot = jnp.where(iota((slots, ROWS), 0, F32) == key, 1.0, 0.0).astype(BF16)
-        return jnp.dot(hot, upd[...], preferred_element_type=F32).astype(BF16)
-
-    def pack_step(k, carry):
-        packed[k] = pack(lax.rem(d + k, n_depth).astype(F32), CAP)
-        return carry
-
-    lax.fori_loop(1, n_depth, pack_step, 0)
-    movers[0] = pack(8.0, MIG)
-    movers[1] = pack(9.0, MIG)
-    own = pl.multiple_of(d * CAP, CAP)
-    spec_out[pl.ds(own, CAP), :] = pack(d.astype(F32), CAP)
+    pl.when(later | (d == 0))(species_work)
 
     def send_block(k):
-        copy = pltpu.make_async_remote_copy(
+        return pltpu.make_async_remote_copy(
             src_ref=packed.at[k],
             dst_ref=spec_out.at[pl.ds(own, CAP), :],
             send_sem=a2a_send.at[k],
@@ -234,10 +247,16 @@
             device_id=at(0, k),
             device_id_type=MESH,
         )
+
+    blocks = [send_block(k) for k in (4, 3, 5, 2, 6, 1, 7)]
+
+    def start_rest():
+        for copy in blocks[3:]:
+            copy.start()
+
+    for copy in blocks[:3]:
         copy.start()
-        return copy
-
-    blocks = [send_block(k) for k in (4, 3, 5)]
+    pl.when(s < 4)(start_rest)
 
     lane = iota((1, 128), 1)
     first_lane = lane == 0
@@ -292,10 +311,6 @@
     loop(6, 10, lambda x: sweep(vbuf, wbuf, x))
     loop(7, 9, residual)
 
-    for i in (0, 1, 4, 5, 6, 7):
-        first[i].wait_recv()
-        second[i].wait_recv()
-
     def fill_plane(x, value, taken):
         value = value.astype(F32)
         for z in range(4):
@@ -306,24 +321,43 @@
                 tbuf[x, z, 12:44, :] = value[:, z * 128:(z + 1) * 128]
         fill_rows(x, taken is not None)
 
-    fill_plane(0, xr_low[0], None)
-    fill_plane(15, xr_high[3], None)
-
-    def fill_outer(i):
-        fill_plane(i, xr_low[i], xs_low[i])
-        fill_plane(11 + i, xr_high[i - 1], xs_high[i - 1])
-
-    loop(1, 4, fill_outer)
-
     def both(step, offset):
         def run(x):
             step(x)
             step(x + offset)
         return run
 
-    loop(1, 5, both(lambda x: sweep(ubuf, vbuf, x), 10))
-    loop(2, 6, both(lambda x: sweep(vbuf, wbuf, x), 8))
-    loop(4, 7, both(residual, 5))
+    def low_side():
+        for i in (0, 4, 5):
+            first[i].wait_recv()
+            second[i].wait_recv()
+        fill_plane(0, xr_low[0], None)
+        for i in range(1, 4):
+            fill_plane(i, xr_low[i], xs_low[i])
+        loop(1, 3, both(lambda x: sweep(ubuf, vbuf, x), 2))
+        loop(2, 4, both(lambda x: sweep(vbuf, wbuf, x), 2))
+        loop(4, 7, residual)
+
+    def high_side():
+        for i in (1, 6, 7):
+            first[i].wait_recv()
+            second[i].wait_recv()
+        fill_plane(15, xr_high[3], None)
+        for i in range(0, 3):
+            fill_plane(12 + i, xr_high[i], xs_high[i])
+        loop(11, 13, both(lambda x: sweep(ubuf, vbuf, x), 2))
+        loop(10, 12, both(lambda x: sweep(vbuf, wbuf, x), 2))
+        loop(9, 12, residual)
+
+    @pl.when(s == n_slab - 1)
+    def _():
+        low_side()
+        high_side()
+
+    @pl.when(s < n_slab - 1)
+    def _():
+        high_side()
+        low_side()
 
     def pair_sum(p, z):
         total = None
@@ -349,7 +383,7 @@
          yc_low.at[pl.ds(0, 4)], yc_high.at[pl.ds(0, 4)],
          yc_low.at[pl.ds(8, 4)], yc_high.at[pl.ds(8, 4)]],
     )
-    blocks += [send_block(k) for k in (2, 6, 1, 7)]
+    pl.when(s >= 4)(start_rest)
     moved = []
     for i, step in enumerate((1, -1)):
         copy = pltpu.make_async_remote_copy(
@@ -462,7 +496,7 @@
         ((2, MIG, WIDTH), BF16), ((6, 2, 48, 128), F32),
         ((16, 4, 56, 128), F32), ((16, 4, 56, 128), F32), ((16, 4, 56, 128), F32),
         ((16, 4, 56, 128), F32), ((8, 4, 32, 128), F32),
-        ((12, 2, 40, 128), F32), ((12, 2, 40, 128), F32), ((12, 2, 40, 128), F32),
+        ((12, 2, 40, 128), F32), ((12, 2, 40, 128), F32), ((12, 2, 40, 128), F32), (row, F32),
     ]
     placed, species_next, order = pl.pallas_call(
         functools.partial(kernel, n_slab, n_depth),

time: 36.2 us -> 35.7 us (0.986)
  the two profiles are of different devices: /device:TPU:1 before, /device:TPU:24 now
where the time goes in v4:
time: 35.7 us; the launch traced here: 35.6 us
  Pallas kernels  34.9 us (98%)
  between operations  0.64 us (2%)
    pallas_call x1, Pallas kernels, local(): pl.pallas_call(functools.partial(kernel, n_slab, n_depth), out_shape=(jax...  33.7 us
    pallas_call x1, Pallas kernels, local(): pl.pallas_call(finish, out_shape=(jax.ShapeDtypeStruct((8, 32, 512), F32)...  1.2 us

profile of v4, /device:TPU:24, one launch (start us, length us, event | category | flops | bytes accessed | tf_op | source)
XLA Modules:
  0.0 35.6 jit_solution(6515039514712393108)
XLA Ops:
  0.6 33.7 %step.1 = (f32[8,32,512]{2,1,0:T(8,128)S(1)}, bf16[2304,128]{1,0:T(8,128)(2,1)S(1)}, bf16[512,512]{1,0:T(8,128)(2,1)S(1)}) custom-call(f32[8,32,512]{2,1,0:T(8,128)} %nut_in.1, bf16[1024,128]{1,0:T(8,128)(2,1)} %spec_in.1, s32[1,1024]{1,0:T(1,128)} %bitcast.7, s32[1,1024]{1,0:T(1,128)} %bitcast.8, s32[1,1024]{1,0:T(1,128)} %bitcast.9, s32[1,1024]{1,0:T(1,128)} %bitcast.10, ...), custom_call_target="tpu_custom_call" | custom-call | tf_op jit(solution)/shard_map/step/pallas_call | solution.py:501
  34.4 1.2 %finish.1 = (f32[8,32,512]{2,1,0:T(8,128)}, bf16[2304,128]{1,0:T(8,128)(2,1)}) custom-call(f32[8,32,512]{2,1,0:T(8,128)S(1)} %get-tuple-element.5.placed, bf16[2304,128]{1,0:T(8,128)(2,1)S(1)} %get-tuple-element.6.species_next, bf16[512,512]{1,0:T(8,128)(2,1)S(1)} %get-tuple-element.7.order), custom_call_target="tpu_custom_call" | custom-call | tf_op jit(solution)/shard_map/finish/pallas_call | solution.py:525

commit v5 on v4

--- a/solution.py
+++ b/solution.py
@@ -221,6 +221,28 @@
          ys_low.at[pl.ds(2, 2)], ys_high.at[pl.ds(2, 2)],
          ys_low.at[pl.ds(12, 2)], ys_high.at[pl.ds(12, 2)]],
     )
+    pl.when(later | (d == 0))(species_work)
+
+    def send_block(k):
+        return pltpu.make_async_remote_copy(
+            src_ref=packed.at[k],
+            dst_ref=spec_out.at[pl.ds(own, CAP), :],
+            send_sem=a2a_send.at[k],
+            recv_sem=a2a_recv.at[k],
+            device_id=at(0, k),
+            device_id_type=MESH,
+        )
+
+    blocks = [send_block(k) for k in (4, 3, 5, 2, 6, 1, 7)]
+
+    def start_rest():
+        for copy in blocks[3:]:
+            copy.start()
+
+    for copy in blocks[:3]:
+        copy.start()
+    pl.when(s < 4)(start_rest)
+
     for half in range(2):
         value = nut[4 * half:4 * half + 4].reshape(128, 512)
         rest = value - value.astype(BF16).astype(F32)
@@ -235,28 +257,6 @@
                 part = value[:, z * 128:(z + 1) * 128]
                 ubuf[4 + x, z, 12:44, :] = part
                 tbuf[4 + x, z, 12:44, :] = SCREENING * part - tbuf[4 + x, z, 12:44, :]
-
-    pl.when(later | (d == 0))(species_work)
-
-    def send_block(k):
-        return pltpu.make_async_remote_copy(
-            src_ref=packed.at[k],
-            dst_ref=spec_out.at[pl.ds(own, CAP), :],
-            send_sem=a2a_send.at[k],
-            recv_sem=a2a_recv.at[k],
-            device_id=at(0, k),
-            device_id_type=MESH,
-        )
-
-    blocks = [send_block(k) for k in (4, 3, 5, 2, 6, 1, 7)]
-
-    def start_rest():
-        for copy in blocks[3:]:
-            copy.start()
-
-    for copy in blocks[:3]:
-        copy.start()
-    pl.when(s < 4)(start_rest)
 
     lane = iota((1, 128), 1)
     first_lane = lane == 0

time: 35.7 us -> 35 us (0.980)
  the two profiles are of different devices: /device:TPU:24 before, /device:TPU:1 now
where the time goes in v5:
time: 35 us; the launch traced here: 34.8 us
  Pallas kernels  34.2 us (98%)
  between operations  0.64 us (2%)
    pallas_call x1, Pallas kernels, local(): pl.pallas_call(functools.partial(kernel, n_slab, n_depth), out_shape=(jax...  33 us
    pallas_call x1, Pallas kernels, local(): pl.pallas_call(finish, out_shape=(jax.ShapeDtypeStruct((8, 32, 512), F32)...  1.21 us

profile of v5, /device:TPU:1, one launch (start us, length us, event | category | flops | bytes accessed | tf_op | source)
XLA Modules:
  0.0 34.8 jit_solution(5183914563483908000)
XLA Ops:
  0.6 33.0 %step.1 = (f32[8,32,512]{2,1,0:T(8,128)S(1)}, bf16[2304,128]{1,0:T(8,128)(2,1)S(1)}, bf16[512,512]{1,0:T(8,128)(2,1)S(1)}) custom-call(f32[8,32,512]{2,1,0:T(8,128)} %nut_in.1, bf16[1024,128]{1,0:T(8,128)(2,1)} %spec_in.1, s32[1,1024]{1,0:T(1,128)} %bitcast.7, s32[1,1024]{1,0:T(1,128)} %bitcast.8, s32[1,1024]{1,0:T(1,128)} %bitcast.9, s32[1,1024]{1,0:T(1,128)} %bitcast.10, ...), custom_call_target="tpu_custom_call" | custom-call | tf_op jit(solution)/shard_map/step/pallas_call | solution.py:501
  33.6 1.2 %finish.1 = (f32[8,32,512]{2,1,0:T(8,128)}, bf16[2304,128]{1,0:T(8,128)(2,1)}) custom-call(f32[8,32,512]{2,1,0:T(8,128)S(1)} %get-tuple-element.5.placed, bf16[2304,128]{1,0:T(8,128)(2,1)S(1)} %get-tuple-element.6.species_next, bf16[512,512]{1,0:T(8,128)(2,1)S(1)} %get-tuple-element.7.order), custom_call_target="tpu_custom_call" | custom-call | tf_op jit(solution)/shard_map/finish/pallas_call | solution.py:525
